TPU v7x, 256 devices: a whole 4x4x8 slice. The times are simulated.
256 devices in a mesh: ep: 16 (over x, y), dp: 16 (over z, core).
Axes of the slice: x: 4, y: 4, z: 8, core: 2. Of those that a mesh axis runs over, the one named last changes fastest.
Arguments:
- tokens: float32 [32768, 1024], P(('ep', 'dp')), may hold values from -6 to 6
- cotangent: float32 [32768, 1024], P(('ep', 'dp')), may hold values from -6 to 6
- w_gate: float32 [256, 1024, 256], P(('ep', 'dp')), may hold values from -0.1875 to 0.1875
- w_up: float32 [256, 1024, 256], P(('ep', 'dp')), may hold values from -0.1875 to 0.1875
- w_down: float32 [256, 256, 1024], P(('ep', 'dp')), may hold values from -0.25 to 0.25
- expert_ids: int32 [32768, 2], P(('ep', 'dp')), may hold values from 0 to 127, as said below
- route_weight: float32 [32768, 2], P(('ep', 'dp')), may hold values from 0.25 to 1
- halted: int32 [32768], P(('ep', 'dp')), may hold values 0 or 1
Outputs:
- grad_x: float32 [32768, 1024], P(('ep', 'dp'))
- grad_gate: float32 [256, 1024, 256], P(('ep', 'dp'))
- grad_up: float32 [256, 1024, 256], P(('ep', 'dp'))
- grad_down: float32 [256, 256, 1024], P(('ep', 'dp'))
Inputs may be any that keep to these rules, and one draw needn't show every extreme that they name: `expert_ids`: within the rows of one device the two ids of a token differ, no expert is named more than 3 times, and every expert whose number is a multiple of 8 is named exactly 3 times.
All inputs are finite; a program needn't handle non-finite values. No bound on the sum of `halted` on one device may be relied on, other than what follows from the above.
Results may differ from a plain program's by a relative error of at most 0.0003.
Values sent between devices are 32-bit elements; how exact they have to be, the bound alone decides.
A program may use at most 128 MiB of HBM per device.

v0:
```python
import jax
import jax.numpy as jnp
from jax import lax
from jax.sharding import PartitionSpec as P

block_rows = 128
highest = lax.Precision.HIGHEST


def expert_grads(x_rows, d_rows, w_gate, w_upper, w_down):
    gate_value = jnp.dot(x_rows, w_gate, precision=highest)
    upper_value = jnp.dot(x_rows, w_upper, precision=highest)
    sigmoid_gate = jax.nn.sigmoid(gate_value)
    active = gate_value * sigmoid_gate
    hidden = active * upper_value
    d_hidden = jnp.dot(d_rows, w_down.T, precision=highest)
    d_gate = d_hidden * upper_value * sigmoid_gate * (1.0 + gate_value * (1.0 - sigmoid_gate))
    d_upper = d_hidden * active
    g_gate = jnp.dot(x_rows.T, d_gate, precision=highest)
    g_upper = jnp.dot(x_rows.T, d_upper, precision=highest)
    g_down = jnp.dot(hidden.T, d_rows, precision=highest)
    d_input = jnp.dot(d_gate, w_gate.T, precision=highest) + jnp.dot(
        d_upper, w_upper.T, precision=highest
    )
    return (g_gate, g_upper, g_down, d_input)


def fill_slots(source, tokens, cotangent, route_rows, flag_rows):
    token_of = source // 2
    x_slots = jnp.take(tokens, token_of, axis=0, mode="fill", fill_value=0.0)
    d_slots = jnp.take(cotangent, token_of, axis=0, mode="fill", fill_value=0.0)
    weights = jnp.take(route_rows, source, axis=0, mode="fill", fill_value=0.0)
    flags = jnp.take(flag_rows, source, axis=0, mode="fill", fill_value=0.0)
    return (x_slots, d_slots * weights[:, None], flags)


def expert_backward(x_rows, d_rows, live_flags, w_gate, w_upper, w_down):
    row_count, model_width = x_rows.shape
    padded = -(-row_count // block_rows) * block_rows
    live_int = (live_flags > 0.5).astype(jnp.int32)
    packed_at = jnp.cumsum(live_int) - live_int
    live_total = jnp.sum(live_int)
    target = jnp.where(live_int > 0, packed_at, padded)
    source = (
        jnp.full((padded + 1,), row_count, jnp.int32)
        .at[target]
        .set(jnp.arange(row_count, dtype=jnp.int32))[:padded]
    )
    packed_x = jnp.take(x_rows, source, axis=0, mode="fill", fill_value=0.0)
    packed_d = jnp.take(d_rows, source, axis=0, mode="fill", fill_value=0.0)
    block_total = (live_total + block_rows - 1) // block_rows
    start_state = (
        jnp.zeros(w_gate.shape, jnp.float32),
        jnp.zeros(w_upper.shape, jnp.float32),
        jnp.zeros(w_down.shape, jnp.float32),
        jnp.zeros((padded, model_width), jnp.float32),
    )

    def block_step(block_index, state):
        block_start = block_index * block_rows
        x_block = lax.dynamic_slice_in_dim(packed_x, block_start, block_rows, 0)
        d_block = lax.dynamic_slice_in_dim(packed_d, block_start, block_rows, 0)
        g_gate, g_upper, g_down, d_input = expert_grads(x_block, d_block, w_gate, w_upper, w_down)
        return (
            state[0] + g_gate,
            state[1] + g_upper,
            state[2] + g_down,
            lax.dynamic_update_slice_in_dim(state[3], d_input, block_start, 0),
        )

    finished = lax.fori_loop(0, block_total, block_step, start_state)
    back_rows = jnp.take(finished[3], jnp.minimum(target, padded - 1), axis=0) * live_int[
        :, None
    ].astype(jnp.float32)
    return (finished[0], finished[1], finished[2], back_rows)


def local(tokens, cotangent, w_gate, w_up, w_down, expert_ids, route_weight, halted):
    ep_count = lax.axis_size("ep")
    dp_count = lax.axis_size("dp")
    token_count, model_width = tokens.shape
    row_total = 2 * token_count
    group_experts = dp_count // 2
    expert_count = ep_count * group_experts
    slot_most = 3 * token_count // expert_count
    flat_ids = expert_ids.reshape(-1)
    owner_index = flat_ids // group_experts
    local_index = flat_ids % group_experts
    one_hot = (flat_ids[:, None] == jnp.arange(expert_count, dtype=jnp.int32)[None, :]).astype(
        jnp.int32
    )
    slot_rank = jnp.sum((jnp.cumsum(one_hot, axis=0) - one_hot) * one_hot, axis=1)
    live_tokens = (1 - halted).astype(jnp.float32)
    route_rows = (route_weight * live_tokens[:, None]).reshape(-1)
    flag_rows = jnp.ones_like(route_rows)
    own_gate = w_gate[0]
    own_upper = w_up[0]
    own_down = w_down[0]
    slot_total = ep_count * dp_count * slot_most
    dest_low = (owner_index * dp_count + 2 * local_index) * slot_most + slot_rank
    dest = jnp.concatenate([dest_low, dest_low + slot_most])
    table = jnp.full((slot_total + 1,), row_total, jnp.int32)
    row_numbers = jnp.arange(row_total, dtype=jnp.int32)
    source = table.at[dest].set(jnp.concatenate([row_numbers, row_numbers]))[:slot_total]
    x_slots, d_slots, f_slots = fill_slots(source, tokens, cotangent, route_rows, flag_rows)
    send_x = x_slots.reshape(ep_count, dp_count, slot_most * model_width)
    send_d = d_slots.reshape(ep_count, dp_count, slot_most * model_width)
    send_f = f_slots.reshape(ep_count, dp_count, slot_most)
    held_x, held_d, held_f = (
        lax.all_to_all(
            lax.all_to_all(send_x, "ep", split_axis=0, concat_axis=0, tiled=True),
            "dp",
            split_axis=1,
            concat_axis=1,
            tiled=True,
        ),
        lax.all_to_all(
            lax.all_to_all(send_d, "ep", split_axis=0, concat_axis=0, tiled=True),
            "dp",
            split_axis=1,
            concat_axis=1,
            tiled=True,
        ),
        lax.all_to_all(
            lax.all_to_all(send_f, "ep", split_axis=0, concat_axis=0, tiled=True),
            "dp",
            split_axis=1,
            concat_axis=1,
            tiled=True,
        ),
    )
    g_gate, g_upper, g_down, back_rows = expert_backward(
        held_x.reshape(-1, model_width),
        held_d.reshape(-1, model_width),
        held_f.reshape(-1),
        own_gate,
        own_upper,
        own_down,
    )
    returned = lax.all_to_all(
        lax.all_to_all(
            back_rows.reshape(ep_count, dp_count, slot_most * model_width),
            "ep",
            split_axis=0,
            concat_axis=0,
            tiled=True,
        ),
        "dp",
        split_axis=1,
        concat_axis=1,
        tiled=True,
    )
    joined = returned.reshape(ep_count, group_experts, 2, slot_most * model_width).sum(axis=2)
    contrib = joined.reshape(ep_count, group_experts, slot_most, model_width)[
        owner_index, local_index, slot_rank
    ]
    grad_x = cotangent + contrib.reshape(token_count, 2, model_width).sum(axis=1)
    return (grad_x, g_gate[None], g_upper[None], g_down[None])


def solution(mesh):
    in_specs = (
        P(("ep", "dp"), None),
        P(("ep", "dp"), None),
        P(("ep", "dp"), None, None),
        P(("ep", "dp"), None, None),
        P(("ep", "dp"), None, None),
        P(("ep", "dp"), None),
        P(("ep", "dp"), None),
        P(("ep", "dp")),
    )
    out_specs = (
        P(("ep", "dp"), None),
        P(("ep", "dp"), None, None),
        P(("ep", "dp"), None, None),
        P(("ep", "dp"), None, None),
    )
    return jax.shard_map(local, mesh=mesh, in_specs=in_specs, out_specs=out_specs, check_vma=False)
```

profile of v0, /device:TPU:1, one launch (start us, length us, event | category | flops | bytes accessed | tf_op | source)
XLA Modules:
  0.0 611.0 jit_solution(17021105274068658303)
XLA Ops:
  6.5 5.0 gather_fusion.6
  11.5 5.0 gather_fusion.2
  17.5 7.6 %all-to-all-start = ((f32[16,16,3]{1,2,0:T(4,128)}), f32[16,16,3]{1,2,0:T(4,128)S(1)}, u32[]{:S(2)}, u32[]{:S(2)}) async-start(f32[16,16,3]{1,2,0:T(4,128)} %copy.66), calls=%async_computation | async-start | bytes 65536 | tf_op jit(solution)/shard_map/all_to_all | solution.py:125
  25.1 3.7 gather_fusion.5
  33.1 9.7 %all-to-all-start.1 = ((f32[16,16,3]{0,2,1:T(4,128)}), f32[16,16,3]{0,2,1:T(4,128)S(1)}, u32[]{:S(2)}, u32[]{:S(2)}) async-start(f32[16,16,3]{0,2,1:T(4,128)} %copy.67), calls=%async_computation.1 | async-start | bytes 65536 | tf_op jit(solution)/shard_map/all_to_all | solution.py:124
  42.9 5.9 select_multiply_fusion
  48.8 4.9 reshape.407
  53.7 6.7 %all-to-all-start.2 = ((f32[16,16,3072]{2,1,0:T(8,128)}), f32[16,16,3072]{2,1,0:T(8,128)}, u32[]{:S(2)}, u32[]{:S(2)}) async-start(f32[16,16,3072]{2,1,0:T(8,128)} %reshape.407), calls=%async_computation.2 | async-start | bytes 6291456 | tf_op jit(solution)/shard_map/all_to_all | solution.py:111
  60.4 5.0 reshape.410
  65.4 36.1 %all-to-all-done.2 = f32[16,16,3072]{2,1,0:T(8,128)} async-done(((f32[16,16,3072]{2,1,0:T(8,128)}), f32[16,16,3072]{2,1,0:T(8,128)}, u32[]{:S(2)}, u32[]{:S(2)}) %all-to-all-start.2) | async-done | bytes 3145760 | tf_op jit(solution)/shard_map/all_to_all | solution.py:111
  101.5 11.9 %all-to-all-start.4 = ((f32[16,16,3072]{2,1,0:T(8,128)}), f32[16,16,3072]{2,1,0:T(8,128)}, u32[]{:S(2)}, u32[]{:S(2)}) async-start(f32[16,16,3072]{2,1,0:T(8,128)} %reshape.410), calls=%async_computation.4 | async-start | bytes 6291456 | tf_op jit(solution)/shard_map/all_to_all | solution.py:118
  113.4 5.3 copy.73
  118.7 34.9 %all-to-all-done.4 = f32[16,16,3072]{2,1,0:T(8,128)} async-done(((f32[16,16,3072]{2,1,0:T(8,128)}), f32[16,16,3072]{2,1,0:T(8,128)}, u32[]{:S(2)}, u32[]{:S(2)}) %all-to-all-start.4) | async-done | bytes 3145760 | tf_op jit(solution)/shard_map/all_to_all | solution.py:118
  153.7 8.6 %all-to-all-start.3 = ((f32[16,16,3072]{2,0,1:T(8,128)}), f32[16,16,3072]{2,0,1:T(8,128)}, u32[]{:S(2)}, u32[]{:S(2)}) async-start(f32[16,16,3072]{2,0,1:T(8,128)} %copy.73), calls=%async_computation.3 | async-start | bytes 6291456 | tf_op jit(solution)/shard_map/all_to_all | solution.py:110
  162.3 5.4 copy.76
  167.7 65.7 %all-to-all-done.3 = f32[16,16,3072]{2,0,1:T(8,128)} async-done(((f32[16,16,3072]{2,0,1:T(8,128)}), f32[16,16,3072]{2,0,1:T(8,128)}, u32[]{:S(2)}, u32[]{:S(2)}) %all-to-all-start.3) | async-done | bytes 3145760 | tf_op jit(solution)/shard_map/all_to_all | solution.py:110
  233.3 5.8 all-to-all-start.5
  244.8 6.1 %mul.148 = f32[16,16,3072]{2,1,0:T(8,128)} reshape(f32[16,16,3,1024]{3,2,1,0:T(4,128)} %mul.147) | data formatting | bytes 6291456 | tf_op jit(solution)/shard_map/mul | solution.py:72
  258.5 5.3 copy.74
  263.9 4.7 reshape.408
  268.5 41.5 %all-to-all-done.5 = f32[16,16,3072]{2,0,1:T(8,128)} async-done(((f32[16,16,3072]{2,0,1:T(8,128)}), f32[16,16,3072]{2,0,1:T(8,128)}, u32[]{:S(2)}, u32[]{:S(2)}) %all-to-all-start.5) | async-done | bytes 3145760 | tf_op jit(solution)/shard_map/all_to_all | solution.py:117
  310.0 5.4 copy.77
  315.4 4.6 reshape.411
  320.0 6.5 %gather_fusion.4 = f32[768,1024]{1,0:T(8,128)} fusion(f32[768,1024]{1,0:T(8,128)} %reshape.408, s32[1024]{0:T(1024)S(1)} %pad_clamp_fusion.1), kind=kCustom, calls=%fused_computation.2.clone | custom fusion | bytes 6294528 | tf_op jit(solution)/shard_map/jit(_take)/gather | solution.py:49
  326.5 6.6 %gather_fusion.7 = f32[768,1024]{1,0:T(8,128)} fusion(f32[768,1024]{1,0:T(8,128)} %reshape.411, s32[1024]{0:T(1024)S(1)} %pad_clamp_fusion.1), kind=kCustom, calls=%fused_computation.5.clone | custom fusion | bytes 6294528 | tf_op jit(solution)/shard_map/jit(_take)/gather | solution.py:50
  333.1 5.9 broadcast_select_fusion
  344.3 113.1 %while.16 = (s32[]{:T(128)}, f32[1024,256]{1,0:T(8,128)}, f32[1024,256]{1,0:T(8,128)}, f32[256,1024]{1,0:T(8,128)}, f32[768,1024]{1,0:T(8,128)}, /*index=5*/s32[...) while((s32[]{:T(128)}, f32[1024,256]{1,0:T(8,128)}, ...), condition=%wide.region_9.13_spmd, body=%wide.region_8.12_spmd.sunk | while | flops 3223224320 | bytes 39190884 | solution.py:71
  457.4 6.6 %gather_fusion = f32[768,1024]{1,0:T(8,128)} fusion(f32[768,1024]{1,0:T(8,128)} %get-tuple-element.68, s32[1024]{0:T(1024)S(1)} %pad_clamp_fusion), kind=kCustom, calls=%fused_computation.6 | custom fusion | bytes 6294528 | tf_op jit(solution)/shard_map/jit(_take)/gather | solution.py:72
  464.0 5.0 gather.19
  472.4 41.6 %all_to_all.40 = f32[16,16,3072]{2,1,0:T(8,128)S(1)} all-to-all(f32[16,16,3072]{2,1,0:T(8,128)S(1)} %select_multiply_fusion.1), channel_id=1, replica_groups=mesh['ep'=16,'dp'=16] {'ep'}, dimensions={0} | all-to-all | bytes 6291456 | tf_op jit(solution)/shard_map/all_to_all | solution.py:141
  517.5 7.4 %all-to-all-start.7 = ((f32[16,16,3072]{2,0,1:T(8,128)}), f32[16,16,3072]{2,0,1:T(8,128)}, u32[]{:S(2)}, u32[]{:S(2)}) async-start(f32[16,16,3072]{2,0,1:T(8,128)} %copy.79), calls=%async_computation.7 | async-start | bytes 6291456 | tf_op jit(solution)/shard_map/all_to_all | solution.py:140
  525.1 70.9 %all-to-all-done.7 = f32[16,16,3072]{2,0,1:T(8,128)} async-done(((f32[16,16,3072]{2,0,1:T(8,128)}), f32[16,16,3072]{2,0,1:T(8,128)}, u32[]{:S(2)}, u32[]{:S(2)}) %all-to-all-start.7) | async-done | bytes 3145760 | tf_op jit(solution)/shard_map/all_to_all | solution.py:140
  (196 shorter events, 162.9 us)
Async XLA Ops:
  0.6 28.2 %copy-start = (f32[128,1024]{1,0:T(8,128)S(1)}, f32[128,1024]{1,0:T(8,128)}, u32[]{:S(2)}) copy-start(f32[128,1024]{1,0:T(8,128)} %param.16) | copy-start | bytes 1572868
  11.5 13.6 %copy-start.2 = (f32[128,1024]{1,0:T(8,128)S(1)}, f32[128,1024]{1,0:T(8,128)}, u32[]{:S(2)}) copy-start(f32[128,1024]{1,0:T(8,128)} %param.17) | copy-start | bytes 1572868
  17.5 14.9 %all-to-all-start = ((f32[16,16,3]{1,2,0:T(4,128)}), f32[16,16,3]{1,2,0:T(4,128)S(1)}, u32[]{:S(2)}, u32[]{:S(2)}) async-start(f32[16,16,3]{1,2,0:T(4,128)} %copy.66), calls=%async_computation | async-start | bytes 65536 | tf_op jit(solution)/shard_map/all_to_all | solution.py:125
  33.1 20.5 %all-to-all-start.1 = ((f32[16,16,3]{0,2,1:T(4,128)}), f32[16,16,3]{0,2,1:T(4,128)S(1)}, u32[]{:S(2)}, u32[]{:S(2)}) async-start(f32[16,16,3]{0,2,1:T(4,128)} %copy.67), calls=%async_computation.1 | async-start | bytes 65536 | tf_op jit(solution)/shard_map/all_to_all | solution.py:124
  53.7 47.8 %all-to-all-start.2 = ((f32[16,16,3072]{2,1,0:T(8,128)}), f32[16,16,3072]{2,1,0:T(8,128)}, u32[]{:S(2)}, u32[]{:S(2)}) async-start(f32[16,16,3072]{2,1,0:T(8,128)} %reshape.407), calls=%async_computation.2 | async-start | bytes 6291456 | tf_op jit(solution)/shard_map/all_to_all | solution.py:111
  101.5 52.2 %all-to-all-start.4 = ((f32[16,16,3072]{2,1,0:T(8,128)}), f32[16,16,3072]{2,1,0:T(8,128)}, u32[]{:S(2)}, u32[]{:S(2)}) async-start(f32[16,16,3072]{2,1,0:T(8,128)} %reshape.410), calls=%async_computation.4 | async-start | bytes 6291456 | tf_op jit(solution)/shard_map/all_to_all | solution.py:118
  153.7 79.7 %all-to-all-start.3 = ((f32[16,16,3072]{2,0,1:T(8,128)}), f32[16,16,3072]{2,0,1:T(8,128)}, u32[]{:S(2)}, u32[]{:S(2)}) async-start(f32[16,16,3072]{2,0,1:T(8,128)} %copy.73), calls=%async_computation.3 | async-start | bytes 6291456 | tf_op jit(solution)/shard_map/all_to_all | solution.py:110
  233.3 76.7 %all-to-all-start.5 = ((f32[16,16,3072]{2,0,1:T(8,128)}), f32[16,16,3072]{2,0,1:T(8,128)}, u32[]{:S(2)}, u32[]{:S(2)}) async-start(f32[16,16,3072]{2,0,1:T(8,128)} %copy.76), calls=%async_computation.5 | async-start | bytes 6291456 | tf_op jit(solution)/shard_map/all_to_all | solution.py:117
  339.1 5.3 copy-start.3
  339.1 5.3 copy-start.4
  344.5 3.5 copy-start.9
  348.0 5.5 copy-start.5
  351.6 4.5 copy-start.7
  363.4 3.5 copy-start.9
  366.8 5.5 copy-start.5
  370.3 4.6 copy-start.7
  382.2 3.5 copy-start.9
  385.6 5.6 copy-start.5
  389.1 4.6 copy-start.7
  393.7 2.9 copy-start.6
  401.0 3.5 copy-start.9
  404.5 5.6 copy-start.5
  408.0 4.6 copy-start.7
  419.8 3.5 copy-start.9
  423.3 5.5 copy-start.5
  426.8 4.6 copy-start.7
  438.6 3.5 copy-start.9
  442.1 5.5 copy-start.5
  445.6 4.6 copy-start.7
  464.0 5.0 copy-start.10
  517.5 78.4 %all-to-all-start.7 = ((f32[16,16,3072]{2,0,1:T(8,128)}), f32[16,16,3072]{2,0,1:T(8,128)}, u32[]{:S(2)}, u32[]{:S(2)}) async-start(f32[16,16,3072]{2,0,1:T(8,128)} %copy.79), calls=%async_computation.7 | async-start | bytes 6291456 | tf_op jit(solution)/shard_map/all_to_all | solution.py:140
  603.3 7.3 %copy-start.1 = (f32[128,1024]{1,0:T(8,128)S(1)}, f32[128,1024]{1,0:T(8,128)}, u32[]{:S(2)}) copy-start(f32[128,1024]{1,0:T(8,128)} %param.16) | copy-start | bytes 1572868
  (11 other events, 20.2 us)
where the time goes:
time: 622 us; the launch traced here: 611 us
  waiting for transfers between devices  249 us (40%)
  local copies, waits for them, and re-layouts  131 us (21%)
  matrix products  106 us (17%)
  starting transfers between devices  57.7 us (9%)
  blocking collectives  41.6 us (7%)
  other arithmetic  22.7 us (4%)
    all_to_all x1, waiting for transfers between devices, local(): lax.all_to_all(lax.all_to_all(back_rows.reshape(ep_count, dp_count, slot_...  70.9 us
    all_to_all x1, waiting for transfers between devices, local(): lax.all_to_all(lax.all_to_all(send_x, 'ep', split_axis=0, concat_axis=0,...  65.7 us
    all_to_all x1, blocking collectives, local(): lax.all_to_all(back_rows.reshape(ep_count, dp_count, slot_most * model_wi...  41.6 us
    all_to_all x1, waiting for transfers between devices, local(): lax.all_to_all(lax.all_to_all(send_d, 'ep', split_axis=0, concat_axis=0,...  41.5 us
    all_to_all x1, waiting for transfers between devices, local(): lax.all_to_all(send_x, 'ep', split_axis=0, concat_axis=0, tiled=True)  36.1 us
    all_to_all x1, waiting for transfers between devices, local(): lax.all_to_all(send_d, 'ep', split_axis=0, concat_axis=0, tiled=True)  34.9 us
    dot_general x6, matrix products, expert_grads(): g_down = jnp.dot(hidden.T, d_rows, precision=highest)  20.4 us
    dot_general x6, matrix products, expert_grads(): g_upper = jnp.dot(x_rows.T, d_upper, precision=highest)  17.1 us
  transfers between devices with their start and end apart: 7, of which 5 were waited for; matrix products, arithmetic and copies ran while one was open for 10% of the time, Pallas kernels for 0%

commit v1 on v0

v1 whole, which is shorter than its diff:
```python
import functools

import jax
import jax.numpy as jnp
from jax import lax
from jax.experimental import pallas as pl
from jax.experimental.pallas import tpu as pltpu
from jax.sharding import PartitionSpec as P

MESH = pl.DeviceIdType.MESH
MOST = 3
GROUPS = 4
LANES = 128
SUB = 8
F32 = jnp.float32
BF16 = jnp.bfloat16


def split(value):
    high = value.astype(BF16)
    return high, (value - high.astype(F32)).astype(BF16)


def dot3(a, b, a_dim, b_dim):
    def dot(p, q):
        return lax.dot_general(p, q, (((a_dim,), (b_dim,)), ((), ())), preferred_element_type=F32)

    return dot(a[0], b[0]) + dot(a[0], b[1]) + dot(a[1], b[0])


def kernel(
    nx,
    ny,
    nz,
    src_ref,
    wgt_ref,
    slot_ref,
    tok_ref,
    cot_ref,
    wg_ref,
    wu_ref,
    wd_ref,
    gx_ref,
    og_ref,
    ou_ref,
    od_ref,
    sbuf,
    rbuf,
    tbuf,
    bbuf,
    xg,
    xu,
    xd,
    gh,
    gl,
    uh,
    ul,
    dh,
    dl,
    ag,
    au,
    ad,
    rg,
    ru,
    rd,
    xh,
    xl,
    eh,
    el,
    send_sem,
    recv_sem,
    back_send_sem,
    back_recv_sem,
    pair_send_sem,
    pair_recv_sem,
):
    ep = lax.axis_index("ep")
    dp = lax.axis_index("dp")
    my_x, my_y = ep // ny, ep % ny
    my_z, my_c = dp // 2, dp % 2
    plane = nx * ny
    per_group = 2 * plane
    total = nz * plane
    half = wg_ref.shape[1]
    rows = per_group * MOST
    partner = (ep, my_z * 2 + 1 - my_c)

    def offset(k):
        group, low = k // per_group, k % per_group
        far, cell = low // plane, low % plane
        dz = (1 - far) * ((4 - group) % 4) + far * (4 + group)
        return cell // ny, cell % ny, dz

    def ahead(k):
        dx, dy, dz = offset(k)
        return ((my_x + dx) % nx) * ny + (my_y + dy) % ny, ((my_z + dz) % nz) * 2 + my_c

    def behind(k):
        dx, dy, dz = offset(k)
        return ((my_x + nx - dx) % nx) * ny + (my_y + ny - dy) % ny, ((my_z + nz - dz) % nz) * 2 + my_c

    barrier = pltpu.get_barrier_semaphore()

    @pl.loop(1, total)
    def _(k):
        pl.semaphore_signal(barrier, inc=1, device_id=ahead(k), device_id_type=MESH)

    pl.semaphore_signal(barrier, inc=1, device_id=partner, device_id_type=MESH)

    def gather(group):
        @pl.loop(0, per_group)
        def _(i):
            k = group * per_group + i
            for r in range(MOST):
                token = src_ref[k * MOST + r]
                sbuf[k, r] = tok_ref[token]
                sbuf[k, MOST + r] = cot_ref[token] * wgt_ref[k * MOST + r]

    def forward(k, group):
        return pltpu.make_async_remote_copy(
            src_ref=sbuf.at[k],
            dst_ref=rbuf.at[k],
            send_sem=send_sem,
            recv_sem=recv_sem.at[group],
            device_id=ahead(k),
            device_id_type=MESH,
        )

    def own_forward():
        return pltpu.make_async_copy(sbuf.at[0], rbuf.at[0], recv_sem.at[0])

    def send(group):
        @pl.loop(1 if group == 0 else 0, per_group)
        def _(i):
            forward(group * per_group + i, group).start()

        if group == 0:
            own_forward().start()

    def to_partner(i, src, dst):
        return pltpu.make_async_remote_copy(
            src_ref=src,
            dst_ref=dst,
            send_sem=pair_send_sem.at[i],
            recv_sem=pair_recv_sem.at[i],
            device_id=partner,
            device_id_type=MESH,
        )

    gather(0)
    gather(1)
    pl.semaphore_wait(barrier, total)
    send(0)
    gather(2)
    send(1)
    gather(3)
    send(2)

    weight_copies = [to_partner(0, wg_ref, xg), to_partner(1, wu_ref, xu), to_partner(2, wd_ref, xd)]
    for copy in weight_copies:
        copy.start()
    send(3)

    gh[:, :half], gl[:, :half] = split(wg_ref[...])
    uh[:, :half], ul[:, :half] = split(wu_ref[...])
    dh[:half, :], dl[:half, :] = split(wd_ref[...])
    for ref in (og_ref, ou_ref, od_ref, ag, au, ad):
        ref[...] = jnp.zeros_like(ref)
    for copy in weight_copies:
        copy.wait()
    gh[:, half:], gl[:, half:] = split(xg[...])
    uh[:, half:], ul[:, half:] = split(xu[...])
    dh[half:, :], dl[half:, :] = split(xd[...])

    flat_in = rbuf.reshape(total * 2 * MOST * SUB, LANES)
    flat_out = tbuf.reshape(total * MOST * SUB, LANES)

    def back(k):
        return pltpu.make_async_remote_copy(
            src_ref=tbuf.at[k],
            dst_ref=bbuf.at[k],
            send_sem=back_send_sem,
            recv_sem=back_recv_sem,
            device_id=behind(k),
            device_id_type=MESH,
        )

    def own_back():
        return pltpu.make_async_copy(tbuf.at[0], bbuf.at[0], back_recv_sem)

    @pl.loop(0, GROUPS)
    def _(group):
        first = group * per_group
        block = pl.ds(first, per_group)
        pltpu.make_async_copy(rbuf.at[block], rbuf.at[block], recv_sem.at[group]).wait()
        for r in range(MOST):
            for lane in range(xh.shape[1] // LANES):
                at = (pl.ds(r * per_group, per_group), pl.ds(lane * LANES, LANES))
                start = first * 2 * MOST * SUB + r * SUB + lane
                part = flat_in[pl.ds(start, per_group, stride=2 * MOST * SUB), :]
                xh[at], xl[at] = split(part)
                part = flat_in[pl.ds(start + MOST * SUB, per_group, stride=2 * MOST * SUB), :]
                eh[at], el[at] = split(part)
        x = (xh[...], xl[...])
        e = (eh[...], el[...])
        gate = dot3(x, (gh[...], gl[...]), 1, 0)
        upper = dot3(x, (uh[...], ul[...]), 1, 0)
        d_hidden = dot3(e, (dh[...], dl[...]), 1, 1)
        sig = jax.nn.sigmoid(gate)
        act = gate * sig
        hidden = split(act * upper)
        d_gate = split(d_hidden * upper * sig * (1.0 + gate * (1.0 - sig)))
        d_upper = split(d_hidden * act)
        d_in = dot3(d_gate, (gh[...], gl[...]), 1, 1) + dot3(d_upper, (uh[...], ul[...]), 1, 1)
        for r in range(MOST):
            for lane in range(xh.shape[1] // LANES):
                start = first * MOST * SUB + r * SUB + lane
                flat_out[pl.ds(start, per_group, stride=MOST * SUB), :] = d_in[
                    r * per_group : (r + 1) * per_group, lane * LANES : (lane + 1) * LANES
                ]
        d_gg = dot3(x, d_gate, 0, 0)
        d_uu = dot3(x, d_upper, 0, 0)
        d_dd = dot3(hidden, e, 0, 0)
        ag[...] += d_gg[:, half:]
        au[...] += d_uu[:, half:]
        ad[...] += d_dd[half:, :]
        og_ref[...] += d_gg[:, :half]
        ou_ref[...] += d_uu[:, :half]
        od_ref[...] += d_dd[:half, :]

        @pl.when(group == 0)
        def _():
            own_back().start()

        @pl.loop(jnp.where(group == 0, 1, 0), per_group)
        def _(i):
            back(first + i).start()

    grad_copies = [to_partner(3, ag, rg), to_partner(4, au, ru), to_partner(5, ad, rd)]
    for copy in grad_copies:
        copy.start()
    for copy, out, got in zip(grad_copies, (og_ref, ou_ref, od_ref), (rg, ru, rd)):
        copy.wait()
        out[...] += got[...]

    pltpu.make_async_copy(bbuf, bbuf, back_recv_sem).wait()

    @pl.loop(0, tok_ref.shape[0])
    def _(t):
        first, second = slot_ref[2 * t], slot_ref[2 * t + 1]
        a = bbuf[first // MOST, first % MOST]
        b = bbuf[second // MOST, second % MOST]
        gx_ref[t] = cot_ref[t] + (a + b)

    others = pl.ds(1, total - 1)
    pltpu.make_async_copy(sbuf.at[others], sbuf.at[others], send_sem).wait()
    pltpu.make_async_copy(tbuf.at[others], tbuf.at[others], back_send_sem).wait()


def local(nx, ny, nz, tokens, cotangent, w_gate, w_up, w_down, expert_ids, route_weight, halted):
    token_count, width = tokens.shape
    half = w_gate.shape[2]
    plane = nx * ny
    total = nx * ny * nz
    slots = total * MOST
    ep = lax.axis_index("ep")
    my_z = lax.axis_index("dp") // 2
    expert = expert_ids.reshape(-1)
    pairs = expert.shape[0]
    row = jnp.arange(pairs, dtype=jnp.int32)
    earlier = (expert[:, None] == expert[None, :]) & (row[None, :] < row[:, None])
    rank = jnp.sum(earlier.astype(jnp.int32), axis=1)
    to_ep, to_z = expert // nz, expert % nz
    dx = (to_ep // ny - ep // ny + nx) % nx
    dy = (to_ep % ny - ep % ny + ny) % ny
    dz = (to_z - my_z + nz) % nz
    group = jnp.where(dz >= 4, dz - 4, (4 - dz) % 4)
    far = jnp.where(dz >= 4, 1, 0)
    place = group * (2 * plane) + far * plane + dx * ny + dy
    slot = place * MOST + rank
    hit = slot[None, :] == jnp.arange(slots, dtype=jnp.int32)[:, None]
    weight = (route_weight * (1 - halted).astype(F32)[:, None]).reshape(-1)
    src = jnp.sum(jnp.where(hit, (row // 2)[None, :], 0), axis=1)
    wgt = jnp.sum(jnp.where(hit, weight[None, :], 0.0), axis=1)
    per_group = 2 * plane
    rows = per_group * MOST
    tile = (SUB, LANES)
    vmem = pl.BlockSpec(memory_space=pltpu.VMEM)
    smem = pl.BlockSpec(memory_space=pltpu.SMEM)
    grad_x, g_gate, g_upper, g_down = pl.pallas_call(
        functools.partial(kernel, nx, ny, nz),
        out_shape=(
            jax.ShapeDtypeStruct((token_count,) + tile, F32),
            jax.ShapeDtypeStruct((width, half), F32),
            jax.ShapeDtypeStruct((width, half), F32),
            jax.ShapeDtypeStruct((half, width), F32),
        ),
        in_specs=[smem, smem, smem] + [vmem] * 5,
        out_specs=(vmem,) * 4,
        scratch_shapes=[
            pltpu.VMEM((total, 2 * MOST) + tile, F32),
            pltpu.VMEM((total, 2 * MOST) + tile, F32),
            pltpu.VMEM((total, MOST) + tile, F32),
            pltpu.VMEM((total, MOST) + tile, F32),
            pltpu.VMEM((width, half), F32),
            pltpu.VMEM((width, half), F32),
            pltpu.VMEM((half, width), F32),
            pltpu.VMEM((width, 2 * half), BF16),
            pltpu.VMEM((width, 2 * half), BF16),
            pltpu.VMEM((width, 2 * half), BF16),
            pltpu.VMEM((width, 2 * half), BF16),
            pltpu.VMEM((2 * half, width), BF16),
            pltpu.VMEM((2 * half, width), BF16),
            pltpu.VMEM((width, half), F32),
            pltpu.VMEM((width, half), F32),
            pltpu.VMEM((half, width), F32),
            pltpu.VMEM((width, half), F32),
            pltpu.VMEM((width, half), F32),
            pltpu.VMEM((half, width), F32),
            pltpu.VMEM((rows, width), BF16),
            pltpu.VMEM((rows, width), BF16),
            pltpu.VMEM((rows, width), BF16),
            pltpu.VMEM((rows, width), BF16),
            pltpu.SemaphoreType.DMA,
            pltpu.SemaphoreType.DMA((GROUPS,)),
            pltpu.SemaphoreType.DMA,
            pltpu.SemaphoreType.DMA,
            pltpu.SemaphoreType.DMA((6,)),
            pltpu.SemaphoreType.DMA((6,)),
        ],
        compiler_params=pltpu.CompilerParams(
            collective_id=0, has_side_effects=True, vmem_limit_bytes=63 * 1024 * 1024
        ),
    )(
        src,
        wgt,
        slot,
        tokens.reshape((token_count,) + tile),
        cotangent.reshape((token_count,) + tile),
        w_gate[0],
        w_up[0],
        w_down[0],
    )
    return grad_x.reshape(token_count, width), g_gate[None], g_upper[None], g_down[None]


def solution(mesh):
    nx, ny = 4, 4
    nz = mesh.shape["dp"] // 2
    spec2 = P(("ep", "dp"), None)
    spec3 = P(("ep", "dp"), None, None)
    return jax.shard_map(
        functools.partial(local, nx, ny, nz),
        mesh=mesh,
        in_specs=(spec2, spec2, spec3, spec3, spec3, spec2, spec2, P(("ep", "dp"))),
        out_specs=(spec2, spec3, spec3, spec3),
        check_vma=False,
    )
```

time: 622 us -> 145 us (0.23); the launches traced: 611 us -> 145 us
  waiting for transfers between devices: 249 us -> 0 us
  Pallas kernels: 0 us -> 131 us
  local copies, waits for them, and re-layouts: 131 us -> 11.4 us
  matrix products: 106 us -> 0 us
  starting transfers between devices: 57.7 us -> 0 us
  blocking collectives: 41.6 us -> 0 us
  other arithmetic: 22.7 us -> 1.68 us
    all_to_all x7 -> x0, waiting for transfers between devices: 249 us -> none  [the longest x1 70.9 us: local(): lax.all_to_all(lax.all_to_all(back_rows.reshape(ep_count, dp_count, slot_...]
    pallas_call x0 -> x1, Pallas kernels: none -> 131 us  [local(): pl.pallas_call(functools.partial(kernel, nx, ny, nz), out_shape=(jax.Shap...]
    dot_general x48 -> x0, matrix products: 106 us -> none  [the longest x6 20.4 us: expert_grads(): g_down = jnp.dot(hidden.T, d_rows, precision=highest)]
    all_to_all x7 -> x0, starting transfers between devices: 57.7 us -> none  [the longest x1 11.9 us: local(): lax.all_to_all(send_d, 'ep', split_axis=0, concat_axis=0, tiled=True)]
    gather x9 -> x0, local copies, waits for them, and re-layouts: 45.3 us -> none  [the longest x2 11.6 us: expert_backward(): jnp.take(finished[3], jnp.minimum(target, padded - 1), axis=0)]
    all_to_all x1 -> x0, blocking collectives: 41.6 us -> none  [local(): lax.all_to_all(back_rows.reshape(ep_count, dp_count, slot_most * model_wi...]
    reshape x12 -> x1, local copies, waits for them, and re-layouts: 27.4 us -> 0.14 us  [local(): expert = expert_ids.reshape(-1)]
    all_to_all x7 -> x0, local copies, waits for them, and re-layouts: 25.8 us -> none  [the longest x1 5.39 us: local(): lax.all_to_all(lax.all_to_all(send_d, 'ep', split_axis=0, concat_axis=0,...]
  transfers between devices with their start and end apart: 7 -> 0, of which waited for: 5 -> 0; matrix products, arithmetic and copies ran while one was open for 10% -> 0% of each run, Pallas kernels for 0% -> 0%
where the time goes in v1:
time: 145 us
  Pallas kernels  131 us (90%)
  local copies, waits for them, and re-layouts  11.4 us (8%)
  other arithmetic  1.68 us (1%)
    pallas_call x1, Pallas kernels, local(): pl.pallas_call(functools.partial(kernel, nx, ny, nz), out_shape=(jax.Shap...  131 us
    unnamed x23, local copies, waits for them, and re-layouts  11 us

profile of v1, /device:TPU:1, one launch (start us, length us, event | category | flops | bytes accessed | tf_op | source)
XLA Modules:
  0.0 144.8 jit_solution(11381829118908744368)
XLA Ops:
  0.7 0.0 copy-start.7
  0.7 0.6 copy-done.7
  1.3 0.0 copy-start.6
  1.3 0.7 copy-done.6
  2.0 0.1 copy.15
  2.1 0.0 copy-start.5
  2.1 0.1 broadcast_in_dim.50
  2.3 0.5 copy-done.5
  2.8 0.1 copy.14
  2.9 0.1 reshape.176
  3.0 0.2 convert_reduce_fusion
  3.3 0.0 copy-start.4
  3.3 0.7 select_reduce_fusion.1.src_ref
  4.0 0.0 copy-done.4
  4.0 0.7 select_reduce_fusion.wgt_ref
  4.7 0.0 copy-start.3
  4.7 2.0 %copy.16 = f32[16,8,8,128]{3,2,1,0:T(8,128)} copy(f32[16,8,8,128]{3,1,2,0:T(8,128)} %bitcast.22) | data formatting | bytes 1048576
  6.7 0.0 copy-done.3
  6.7 0.9 copy.17
  7.6 131.0 %shard_map.111 = (f32[128,8,128]{2,1,0:T(8,128)}, f32[1024,256]{1,0:T(8,128)}, f32[1024,256]{1,0:T(8,128)}, f32[256,1024]{1,0:T(8,128)}) custom-call(s32[384]{0:T(512)} %select_reduce_fusion.1.src_ref, f32[384]{0:T(512)} %select_reduce_fusion.wgt_ref, s32[256]{0:T(256)} %copy-done.4, f32[128,8,128]{2,1,0:T(8,128)} %bitcast.14, f32[128,8,128]{2,1,0:T(8,128)} %bitcast.15, ...), custom_call_target="tpu_custom_call" | custom-call | tf_op jit(solution)/shard_map/pallas_call | solution.py:290
  138.6 0.0 copy-start.2
  138.6 2.0 %copy.20 = f32[16,8,8,128]{3,1,2,0:T(8,128)} copy(f32[16,8,8,128]{3,2,1,0:T(8,128)} %bitcast.25) | data formatting | bytes 1048576
  140.6 0.0 copy-done.2
  140.7 0.0 copy-start.1
  140.7 1.0 copy.24
  141.6 0.6 copy-done.1
  142.3 0.0 copy-start
  142.3 1.0 copy.25
  143.2 0.6 copy-done
  143.9 1.0 copy.26
  (3 shorter events, 0.0 us)
Async XLA Ops:
  0.7 0.7 copy-start.7
  1.3 0.7 copy-start.6
  2.1 0.7 copy-start.5
  3.3 0.7 copy-start.4
  4.7 2.0 %copy-start.3 = (f32[128,1024]{1,0:T(8,128)S(1)}, f32[128,1024]{1,0:T(8,128)}, u32[]{:S(2)}) copy-start(f32[128,1024]{1,0:T(8,128)} %param.9) | copy-start | bytes 1572868
  138.6 2.0 %copy-start.2 = (f32[1024,256]{1,0:T(8,128)S(1)}, f32[1024,256]{1,0:T(8,128)}, u32[]{:S(2)}) copy-start(f32[1024,256]{1,0:T(8,128)} %get-tuple-element.9) | copy-start | bytes 3145732
  140.7 1.6 %copy-start.1 = (f32[1024,256]{1,0:T(8,128)S(1)}, f32[1024,256]{1,0:T(8,128)}, u32[]{:S(2)}) copy-start(f32[1024,256]{1,0:T(8,128)} %get-tuple-element.10) | copy-start | bytes 3145732
  142.3 1.6 %copy-start = (f32[256,1024]{1,0:T(8,128)S(1)}, f32[256,1024]{1,0:T(8,128)}, u32[]{:S(2)}) copy-start(f32[256,1024]{1,0:T(8,128)} %get-tuple-element.11) | copy-start | bytes 3145732

commit v2 on v1

v2 whole, which is shorter than its diff:
```python
import functools

import jax
import jax.numpy as jnp
from jax import lax
from jax.experimental import pallas as pl
from jax.experimental.pallas import tpu as pltpu
from jax.sharding import PartitionSpec as P

MESH = pl.DeviceIdType.MESH
MOST = 3
GROUPS = 4
FIRST = 48
CAPS = ((128, 128, 96, 48), (128, 96, 48))
LANES = 128
SUB = 8
F32 = jnp.float32
BF16 = jnp.bfloat16


def split(value):
    high = value.astype(BF16)
    return high, (value - high.astype(F32)).astype(BF16)


def dot3(a, b, a_dim, b_dim):
    def dot(p, q):
        return lax.dot_general(p, q, (((a_dim,), (b_dim,)), ((), ())), preferred_element_type=F32)

    return dot(a[0], b[0]) + dot(a[0], b[1]) + dot(a[1], b[0])


def kernel(
    nx,
    ny,
    nz,
    ids_ref,
    route_ref,
    halt_ref,
    tok_ref,
    cot_ref,
    wg_ref,
    wu_ref,
    wd_ref,
    gx_ref,
    og_ref,
    ou_ref,
    od_ref,
    tok3,
    cot3,
    turn_a,
    turn_b,
    turn_w,
    list_v,
    list_s,
    row_ref,
    wgt_ref,
    own,
    hops,
    row_in,
    wgt_in,
    row_tab,
    wgt_tab,
    sbuf,
    rbuf,
    tbuf,
    bbuf,
    xg,
    xu,
    xd,
    gh,
    gl,
    uh,
    ul,
    dh,
    dl,
    ag,
    au,
    ad,
    rg,
    ru,
    rd,
    xh,
    xl,
    eh,
    el,
    hop_send_sem,
    hop_recv_sem,
    row_send_sem,
    row_recv_sem,
    wgt_send_sem,
    wgt_recv_sem,
    tab_sem,
    send_sem,
    recv_sem,
    back_send_sem,
    back_recv_sem,
    pair_send_sem,
    pair_recv_sem,
):
    ep = lax.axis_index("ep")
    dp = lax.axis_index("dp")
    my_x, my_y = ep // ny, ep % ny
    my_z, my_c = dp // 2, dp % 2
    sign = 1 - 2 * my_c
    plane = nx * ny
    per_group = 2 * plane
    total = nz * plane
    half = wg_ref.shape[1]
    tokens, width = tok_ref.shape
    low_bits = nz - 1
    partner = (ep, my_z * 2 + 1 - my_c)

    def column(step):
        return ep, ((my_z + nz + step) % nz) * 2 + my_c

    def offset(k):
        group, low = k // per_group, k % per_group
        side, cell = low // plane, low % plane
        hop = group + 1
        dz = jnp.where(side == 0, sign * hop, jnp.where(group == GROUPS - 1, 0, -sign * hop))
        return cell // ny, cell % ny, dz

    def behind(k):
        dx, dy, dz = offset(k)
        return ((my_x + nx - dx) % nx) * ny + (my_y + ny - dy) % ny, ((my_z + nz - dz) % nz) * 2 + my_c

    def beside(cell):
        return ((my_x + cell // ny) % nx) * ny + (my_y + cell % ny) % ny, dp

    barrier = pltpu.get_barrier_semaphore()

    @pl.loop(0, nz)
    def _(other_z):
        @pl.loop(0, plane)
        def _(other):
            @pl.when((other_z != my_z) | (other != ep))
            def _():
                pl.semaphore_signal(barrier, inc=1, device_id=(other, other_z * 2 + my_c), device_id_type=MESH)

    pl.semaphore_signal(barrier, inc=1, device_id=partner, device_id_type=MESH)

    def remote(src, dst, send, recv, device):
        return pltpu.make_async_remote_copy(
            src_ref=src, dst_ref=dst, send_sem=send, recv_sem=recv, device_id=device, device_id_type=MESH
        )

    def toward(side):
        return column(sign if side == 0 else -sign)

    def hop_parts(side, hop):
        cap = CAPS[side][hop]
        return ((0, FIRST), (FIRST, cap)) if cap > FIRST else ((0, cap),)

    def hop_copy(side, hop, part):
        start, end = hop_parts(side, hop)[part]
        rows = pl.ds(start, end - start)
        src = own.at[side, rows] if hop == 0 else hops[side][hop - 1].at[rows]
        return remote(
            src,
            hops[side][hop].at[rows],
            hop_send_sem.at[side, hop, part],
            hop_recv_sem.at[side, hop, part],
            toward(side),
        )

    def table_copies(side, hop):
        device = column(sign * (hop + 1) if side == 0 else -sign * (hop + 1))
        at = 2 * hop + side
        return (
            remote(row_ref.at[at], row_in.at[side, hop], row_send_sem.at[at], row_recv_sem.at[side, hop], device),
            remote(wgt_ref.at[at], wgt_in.at[side, hop], wgt_send_sem.at[at], wgt_recv_sem.at[side, hop], device),
        )

    def block_copy(k, group, cell):
        return remote(sbuf.at[k], rbuf.at[k], send_sem, recv_sem.at[group], beside(cell))

    def send_blocks(group, side):
        first = group * per_group + side * plane
        pltpu.make_async_copy(sbuf.at[first], rbuf.at[first], recv_sem.at[group]).start()

        @pl.loop(1, plane)
        def _(cell):
            block_copy(first + cell, group, cell).start()

    def to_partner(i, src, dst):
        return remote(src, dst, pair_send_sem.at[i], pair_recv_sem.at[i], partner)

    flat_tok = tok3.reshape(tokens * SUB, LANES)
    flat_cot = cot3.reshape(tokens * SUB, LANES)
    for lane in range(SUB):
        at = pl.ds(lane * LANES, LANES)
        to = pl.ds(lane, tokens, stride=SUB)
        flat_tok[to, :] = tok_ref[:, at]
        flat_cot[to, :] = cot_ref[:, at]

    live = 1 - halt_ref[...]
    experts = [ids_ref[pl.ds(j, 1), :] for j in range(2)]
    turned = [(sign * ((e & low_bits) - my_z)) & low_bits for e in experts]
    long_side = [(t >= 1) & (t <= GROUPS) for t in turned]
    short_side = [t > GROUPS for t in turned]
    far = [
        jnp.maximum(*[jnp.where(m, t, 0) for m, t in zip(long_side, turned)]) * live,
        jnp.maximum(*[jnp.where(m, nz - t, 0) for m, t in zip(short_side, turned)]) * live,
    ]
    for ref in (turn_a, turn_b, turn_w):
        ref[...] = jnp.zeros_like(ref)
    list_v[...] = jnp.zeros_like(list_v)
    for i, line in enumerate(experts + far):
        turn_a[pl.ds(i, 1), :] = line
    columns = turn_a[...].T
    below = lax.broadcasted_iota(jnp.int32, (tokens, tokens), 0)
    across = lax.broadcasted_iota(jnp.int32, (tokens, tokens), 1)
    earlier = below < across

    def column_of(matrix, i):
        return matrix[:, i : i + 1]

    def count(mask):
        return jnp.sum(jnp.where(mask, 1, 0), axis=0, keepdims=True)

    lines = [turn_a[pl.ds(i, 1), :] for i in range(4)]
    ranks = [
        count((column_of(columns, 0) == lines[0]) & earlier),
        count((column_of(columns, 1) == lines[1]) & earlier) + count(column_of(columns, 0) == lines[1]),
    ]
    places = []
    for i in (2, 3):
        other = column_of(columns, i)
        places.append(count((other > lines[i]) | ((other == lines[i]) & earlier)))
    lane_index = lax.broadcasted_iota(jnp.int32, (1, tokens), 1)
    shift = nz.bit_length() - 1
    for i in range(2):
        turn_b[pl.ds(i, 1), :] = places[i]
    for j in range(2):
        to_ep = experts[j] >> shift
        dx = ((to_ep >> (ny.bit_length() - 1)) - my_x) & (nx - 1)
        dy = ((to_ep & (ny - 1)) - my_y) & (ny - 1)
        hop = jnp.where(long_side[j], turned[j] - 1, jnp.where(turned[j] == 0, GROUPS - 1, nz - 1 - turned[j]))
        line = 2 * hop + jnp.where(long_side[j], 0, 1)
        within = (dx * ny + dy) * MOST + jnp.minimum(ranks[j], MOST - 1)
        list_v[pl.ds(2 + j, 1), :] = jnp.clip(line * (plane * MOST) + within, 0, total * MOST - 1)
        row = jnp.where(long_side[j], places[0], jnp.where(turned[j] == 0, lane_index, places[1]))
        turn_b[pl.ds(2 + j, 1), :] = line * LANES + within
        turn_b[pl.ds(4 + j, 1), :] = row * live
        turn_w[pl.ds(j, 1), :] = route_ref[pl.ds(j, 1), :] * live.astype(F32)
    columns = turn_b[...].T
    weights = turn_w[...].T
    for i in range(2):
        found = jnp.sum(jnp.where(column_of(columns, i) == across, below, 0), axis=0, keepdims=True)
        list_v[pl.ds(i, 1), :] = jnp.clip(found, 0, tokens - 1)
    pick_lists = pltpu.make_async_copy(list_v, list_s, tab_sem.at[0])
    pick_lists.start()
    for i in range(2 * GROUPS):
        hit = [column_of(columns, 2 + j) == across + i * LANES for j in range(2)]
        row = jnp.sum(
            sum(jnp.where(hit[j], column_of(columns, 4 + j), 0) for j in range(2)), axis=0, keepdims=True
        )
        wgt = jnp.sum(
            sum(jnp.where(hit[j], column_of(weights, j), 0.0) for j in range(2)), axis=0, keepdims=True
        )
        limit = CAPS[i % 2][i // 2] if i // 2 < len(CAPS[i % 2]) else tokens
        row_ref[i] = jnp.broadcast_to(jnp.clip(row, 0, limit - 1), (SUB, LANES))
        wgt_ref[i] = jnp.broadcast_to(wgt, (SUB, LANES))
    pick_lists.wait()

    @pl.loop(0, tokens // SUB)
    def _(block):
        for side in range(2):
            picked = [list_s[side, block * SUB + i] for i in range(SUB)]
            rows = [(tok3[token], cot3[token]) for token in picked]
            for i, (a, b) in enumerate(rows):
                own[side, block * SUB + i, 0] = a
                own[side, block * SUB + i, 1] = b

    last_line = 2 * GROUPS - 1
    own_tables = [
        pltpu.make_async_copy(row_ref.at[last_line], row_tab.at[1, GROUPS - 1], tab_sem.at[0]),
        pltpu.make_async_copy(wgt_ref.at[last_line], wgt_tab.at[1, GROUPS - 1], tab_sem.at[1]),
    ]
    for copy in own_tables:
        copy.start()
    pl.semaphore_wait(barrier, total)
    lanes = [(side, hop) for hop in range(GROUPS) for side in range(2) if hop < len(CAPS[side])]
    for part in range(2):
        for side in range(2):
            hop_copy(side, 0, part).start()
    for side, hop in lanes:
        for copy in table_copies(side, hop):
            copy.start()
    weight_copies = [to_partner(0, wg_ref, xg), to_partner(1, wu_ref, xu), to_partner(2, wd_ref, xd)]
    for copy in weight_copies:
        copy.start()
    for copy in own_tables:
        copy.wait()

    def pick(group, side):
        held = None if (group, side) == (GROUPS - 1, 1) else hops[side][group]

        @pl.loop(0, plane)
        def _(cell):
            k = group * per_group + side * plane + cell
            at = [(row_tab[side, group, 0, cell * MOST + r], wgt_tab[side, group, 0, cell * MOST + r]) for r in range(MOST)]
            if held is None:
                rows = [(tok3[row], cot3[row] * wgt) for row, wgt in at]
            else:
                rows = [(held[row, 0], held[row, 1] * wgt) for row, wgt in at]
            for r, (a, b) in enumerate(rows):
                sbuf[k, r] = a
                sbuf[k, MOST + r] = b

    pick(GROUPS - 1, 1)
    send_blocks(GROUPS - 1, 1)

    gh[:, :half], gl[:, :half] = split(wg_ref[...])
    uh[:, :half], ul[:, :half] = split(wu_ref[...])
    dh[:half, :], dl[:half, :] = split(wd_ref[...])
    for ref in (og_ref, ou_ref, od_ref, ag, au, ad):
        ref[...] = jnp.zeros_like(ref)
    for copy in weight_copies:
        copy.wait()
    gh[:, half:], gl[:, half:] = split(xg[...])
    uh[:, half:], ul[:, half:] = split(xu[...])
    dh[half:, :], dl[half:, :] = split(xd[...])
    for side, hop in lanes:
        for copy in table_copies(side, hop):
            copy.wait_recv()
    tables = [
        pltpu.make_async_copy(table.at[side, pl.ds(0, len(CAPS[side]))], to.at[side, pl.ds(0, len(CAPS[side]))], tab_sem.at[i])
        for i, (table, to, side) in enumerate(
            [(row_in, row_tab, 0), (wgt_in, wgt_tab, 0), (row_in, row_tab, 1), (wgt_in, wgt_tab, 1)]
        )
    ]
    for copy in tables:
        copy.start()
    for copy in tables:
        copy.wait()

    flat_in = rbuf.reshape(total * 2 * MOST * SUB, LANES)
    flat_out = tbuf.reshape(total * MOST * SUB, LANES)

    def back(k):
        return remote(tbuf.at[k], bbuf.at[k], back_send_sem, back_recv_sem, behind(k))

    def compute(group):
        first = group * per_group
        block = pl.ds(first, per_group)
        pltpu.make_async_copy(rbuf.at[block], rbuf.at[block], recv_sem.at[group]).wait()
        for r in range(MOST):
            for lane in range(xh.shape[1] // LANES):
                at = (pl.ds(r * per_group, per_group), pl.ds(lane * LANES, LANES))
                start = first * 2 * MOST * SUB + r * SUB + lane
                part = flat_in[pl.ds(start, per_group, stride=2 * MOST * SUB), :]
                xh[at], xl[at] = split(part)
                part = flat_in[pl.ds(start + MOST * SUB, per_group, stride=2 * MOST * SUB), :]
                eh[at], el[at] = split(part)
        x = (xh[...], xl[...])
        e = (eh[...], el[...])
        gate = dot3(x, (gh[...], gl[...]), 1, 0)
        upper = dot3(x, (uh[...], ul[...]), 1, 0)
        d_hidden = dot3(e, (dh[...], dl[...]), 1, 1)
        sig = jax.nn.sigmoid(gate)
        act = gate * sig
        hidden = split(act * upper)
        d_gate = split(d_hidden * upper * sig * (1.0 + gate * (1.0 - sig)))
        d_upper = split(d_hidden * act)
        d_in = dot3(d_gate, (gh[...], gl[...]), 1, 1) + dot3(d_upper, (uh[...], ul[...]), 1, 1)
        for r in range(MOST):
            for lane in range(xh.shape[1] // LANES):
                start = first * MOST * SUB + r * SUB + lane
                flat_out[pl.ds(start, per_group, stride=MOST * SUB), :] = d_in[
                    r * per_group : (r + 1) * per_group, lane * LANES : (lane + 1) * LANES
                ]
        d_gg = dot3(x, d_gate, 0, 0)
        d_uu = dot3(x, d_upper, 0, 0)
        d_dd = dot3(hidden, e, 0, 0)
        ag[...] += d_gg[:, half:]
        au[...] += d_uu[:, half:]
        ad[...] += d_dd[half:, :]
        og_ref[...] += d_gg[:, :half]
        ou_ref[...] += d_uu[:, :half]
        od_ref[...] += d_dd[:half, :]

        own_block = (GROUPS - 1) * per_group + plane

        @pl.loop(0, per_group)
        def _(i):
            k = first + i

            @pl.when(k != own_block)
            def _():
                back(k).start()

            @pl.when(k == own_block)
            def _():
                pltpu.make_async_copy(tbuf.at[own_block], bbuf.at[own_block], back_recv_sem).start()

    @pl.loop(0, GROUPS + 1)
    def _(step):
        for hop in range(GROUPS):

            @pl.when(step == hop)
            def _():
                for side in range(2):
                    if hop < len(CAPS[side]):
                        for part in range(len(hop_parts(side, hop))):
                            hop_copy(side, hop, part).wait_recv()
                            if hop + 1 < len(CAPS[side]) and part < len(hop_parts(side, hop + 1)):
                                hop_copy(side, hop + 1, part).start()
                for side in range(2):
                    if hop < len(CAPS[side]):
                        pick(hop, side)
                for side in range(2):
                    if hop < len(CAPS[side]):
                        send_blocks(hop, side)

        @pl.when(step >= 1)
        def _():
            compute(step - 1)

    grad_copies = [to_partner(3, ag, rg), to_partner(4, au, ru), to_partner(5, ad, rd)]
    for copy in grad_copies:
        copy.start()
    for copy, out, got in zip(grad_copies, (og_ref, ou_ref, od_ref), (rg, ru, rd)):
        copy.wait()
        out[...] += got[...]

    pltpu.make_async_copy(bbuf, bbuf, back_recv_sem).wait()

    flat_back = bbuf.reshape(total * MOST, SUB, LANES)

    @pl.loop(0, tokens // SUB)
    def _(block):
        found = []
        for i in range(SUB):
            t = block * SUB + i
            found.append(cot3[t] + (flat_back[list_s[2, t]] + flat_back[list_s[3, t]]))
        for i, value in enumerate(found):
            tok3[block * SUB + i] = value

    for lane in range(SUB):
        gx_ref[:, pl.ds(lane * LANES, LANES)] = flat_tok[pl.ds(lane, tokens, stride=SUB), :]

    for side, hop in lanes:
        for part in range(len(hop_parts(side, hop))):
            hop_copy(side, hop, part).wait_send()
        for copy in table_copies(side, hop):
            copy.wait_send()
    sent = pl.ds(0, total - 2 * GROUPS)
    pltpu.make_async_copy(sbuf.at[sent], sbuf.at[sent], send_sem).wait()
    others = pl.ds(0, total - 1)
    pltpu.make_async_copy(tbuf.at[others], tbuf.at[others], back_send_sem).wait()


def local(nx, ny, nz, tokens, cotangent, w_gate, w_up, w_down, expert_ids, route_weight, halted):
    token_count, width = tokens.shape
    half = w_gate.shape[2]
    plane = nx * ny
    total = nx * ny * nz
    rows = 2 * plane * MOST
    tile = (SUB, LANES)
    vmem = pl.BlockSpec(memory_space=pltpu.VMEM)
    dma = pltpu.SemaphoreType.DMA
    grad_x, g_gate, g_upper, g_down = pl.pallas_call(
        functools.partial(kernel, nx, ny, nz),
        out_shape=(
            jax.ShapeDtypeStruct((token_count, width), F32),
            jax.ShapeDtypeStruct((width, half), F32),
            jax.ShapeDtypeStruct((width, half), F32),
            jax.ShapeDtypeStruct((half, width), F32),
        ),
        in_specs=[vmem] * 8,
        out_specs=(vmem,) * 4,
        scratch_shapes=[
            pltpu.VMEM((token_count,) + tile, F32),
            pltpu.VMEM((token_count,) + tile, F32),
            pltpu.VMEM(tile, jnp.int32),
            pltpu.VMEM(tile, jnp.int32),
            pltpu.VMEM(tile, F32),
            pltpu.VMEM(tile, jnp.int32),
            pltpu.SMEM(tile, jnp.int32),
            pltpu.VMEM((2 * GROUPS,) + tile, jnp.int32),
            pltpu.VMEM((2 * GROUPS,) + tile, F32),
            pltpu.VMEM((2, token_count, 2) + tile, F32),
            tuple(tuple(pltpu.VMEM((cap, 2) + tile, F32) for cap in caps) for caps in CAPS),
            pltpu.VMEM((2, GROUPS) + tile, jnp.int32),
            pltpu.VMEM((2, GROUPS) + tile, F32),
            pltpu.SMEM((2, GROUPS) + tile, jnp.int32),
            pltpu.SMEM((2, GROUPS) + tile, F32),
            pltpu.VMEM((total, 2 * MOST) + tile, F32),
            pltpu.VMEM((total, 2 * MOST) + tile, F32),
            pltpu.VMEM((total, MOST) + tile, F32),
            pltpu.VMEM((total, MOST) + tile, F32),
            pltpu.VMEM((width, half), F32),
            pltpu.VMEM((width, half), F32),
            pltpu.VMEM((half, width), F32),
            pltpu.VMEM((width, 2 * half), BF16),
            pltpu.VMEM((width, 2 * half), BF16),
            pltpu.VMEM((width, 2 * half), BF16),
            pltpu.VMEM((width, 2 * half), BF16),
            pltpu.VMEM((2 * half, width), BF16),
            pltpu.VMEM((2 * half, width), BF16),
            pltpu.VMEM((width, half), F32),
            pltpu.VMEM((width, half), F32),
            pltpu.VMEM((half, width), F32),
            pltpu.VMEM((width, half), F32),
            pltpu.VMEM((width, half), F32),
            pltpu.VMEM((half, width), F32),
            pltpu.VMEM((rows, width), BF16),
            pltpu.VMEM((rows, width), BF16),
            pltpu.VMEM((rows, width), BF16),
            pltpu.VMEM((rows, width), BF16),
            dma((2, GROUPS, 2)),
            dma((2, GROUPS, 2)),
            dma((2 * GROUPS,)),
            dma((2, GROUPS)),
            dma((2 * GROUPS,)),
            dma((2, GROUPS)),
            dma((4,)),
            dma,
            dma((GROUPS,)),
            dma,
            dma,
            dma((6,)),
            dma((6,)),
        ],
        compiler_params=pltpu.CompilerParams(
            collective_id=0, has_side_effects=True, vmem_limit_bytes=63 * 1024 * 1024
        ),
    )(
        expert_ids.T,
        route_weight.T,
        halted.reshape(1, token_count),
        tokens,
        cotangent,
        w_gate[0],
        w_up[0],
        w_down[0],
    )
    return grad_x, g_gate[None], g_upper[None], g_down[None]


def solution(mesh):
    nx, ny = 4, 4
    nz = mesh.shape["dp"] // 2
    spec2 = P(("ep", "dp"), None)
    spec3 = P(("ep", "dp"), None, None)
    return jax.shard_map(
        functools.partial(local, nx, ny, nz),
        mesh=mesh,
        in_specs=(spec2, spec2, spec3, spec3, spec3, spec2, spec2, P(("ep", "dp"))),
        out_specs=(spec2, spec3, spec3, spec3),
        check_vma=False,
    )
```

time: 145 us -> 138 us (0.952)
  the two profiles are of different devices: /device:TPU:1 before, /device:TPU:33 now
where the time goes in v2:
time: 138 us
  Pallas kernels  131 us (95%)
  local copies, waits for them, and re-layouts  6.15 us (4%)
    pallas_call x1, Pallas kernels, local(): pl.pallas_call(functools.partial(kernel, nx, ny, nz), out_shape=(jax.Shap...  131 us
    unnamed x10, local copies, waits for them, and re-layouts  6.15 us

profile of v2, /device:TPU:33, one launch (start us, length us, event | category | flops | bytes accessed | tf_op | source)
XLA Modules:
  0.0 137.8 jit_solution(7395381275994297738)
XLA Ops:
  0.6 131.0 %shard_map.111 = (f32[128,1024]{1,0:T(8,128)}, f32[1024,256]{1,0:T(8,128)}, f32[1024,256]{1,0:T(8,128)}, f32[256,1024]{1,0:T(8,128)}) custom-call(s32[2,128]{1,0:T(2,128)} %bitcast.15, f32[2,128]{1,0:T(2,128)} %bitcast.16, s32[1,128]{1,0:T(1,128)} %bitcast.17, f32[128,1024]{1,0:T(8,128)} %tok_ref.1, f32[128,1024]{1,0:T(8,128)} %cot_ref.1, ...), custom_call_target="tpu_custom_call" | custom-call | tf_op jit(solution)/shard_map/pallas_call | solution.py:464
  131.6 0.0 copy-start.2
  131.6 2.0 %copy.16 = f32[128,1024]{1,0:T(8,128)} copy(f32[128,1024]{1,0:T(8,128)} %get-tuple-element.16) | data formatting | bytes 1048576
  133.6 0.0 copy-done.2
  133.6 0.0 copy-start.1
  133.6 1.0 copy.17
  134.6 0.6 copy-done.1
  135.2 0.0 copy-start
  135.2 1.0 copy.18
  136.2 0.6 copy-done
  136.8 1.0 copy.19
Async XLA Ops:
  131.6 2.0 %copy-start.2 = (f32[1024,256]{1,0:T(8,128)S(1)}, f32[1024,256]{1,0:T(8,128)}, u32[]{:S(2)}) copy-start(f32[1024,256]{1,0:T(8,128)} %get-tuple-element.9) | copy-start | bytes 3145732
  133.6 1.6 %copy-start.1 = (f32[1024,256]{1,0:T(8,128)S(1)}, f32[1024,256]{1,0:T(8,128)}, u32[]{:S(2)}) copy-start(f32[1024,256]{1,0:T(8,128)} %get-tuple-element.10) | copy-start | bytes 3145732
  135.2 1.6 %copy-start = (f32[256,1024]{1,0:T(8,128)S(1)}, f32[256,1024]{1,0:T(8,128)}, u32[]{:S(2)}) copy-start(f32[256,1024]{1,0:T(8,128)} %get-tuple-element.11) | copy-start | bytes 3145732

commit v3 on v2

--- a/solution.py
+++ b/solution.py
@@ -46,6 +46,12 @@
     og_ref,
     ou_ref,
     od_ref,
+    wg,
+    wu,
+    wd,
+    og,
+    ou,
+    od,
     tok3,
     cot3,
     turn_a,
@@ -84,6 +90,8 @@
     xl,
     eh,
     el,
+    load_sem,
+    meet_sem,
     hop_send_sem,
     hop_recv_sem,
     row_send_sem,
@@ -106,7 +114,7 @@
     plane = nx * ny
     per_group = 2 * plane
     total = nz * plane
-    half = wg_ref.shape[1]
+    half = wg.shape[1]
     tokens, width = tok_ref.shape
     low_bits = nz - 1
     partner = (ep, my_z * 2 + 1 - my_c)
@@ -130,15 +138,32 @@
 
     barrier = pltpu.get_barrier_semaphore()
 
-    @pl.loop(0, nz)
-    def _(other_z):
-        @pl.loop(0, plane)
-        def _(other):
-            @pl.when((other_z != my_z) | (other != ep))
-            def _():
-                pl.semaphore_signal(barrier, inc=1, device_id=(other, other_z * 2 + my_c), device_id_type=MESH)
-
-    pl.semaphore_signal(barrier, inc=1, device_id=partner, device_id_type=MESH)
+    def at_xy(dx, dy):
+        return ((my_x + nx + dx) % nx) * ny + (my_y + ny + dy) % ny, dp
+
+    rings = (
+        (column(1), column(-1)),
+        (at_xy(1, 0), at_xy(-1, 0)),
+        (at_xy(0, 1), at_xy(0, -1)),
+    )
+    for device in [device for ring in rings for device in ring] + [partner]:
+        pl.semaphore_signal(barrier, inc=1, device_id=device, device_id_type=MESH)
+
+    weight_loads = [
+        pltpu.make_async_copy(src, dst, load_sem.at[i])
+        for i, (src, dst) in enumerate([(wg_ref, wg), (wu_ref, wu), (wd_ref, wd)])
+    ]
+    for copy in weight_loads:
+        copy.start()
+
+    def meet():
+        turn = 0
+        for ring, length in zip(rings, (nz, nx, ny)):
+            for _ in range(length // 2 - (1 if length == nz else 0)):
+                for device in ring:
+                    pl.semaphore_signal(meet_sem.at[turn], inc=1, device_id=device, device_id_type=MESH)
+                pl.semaphore_wait(meet_sem.at[turn], 2)
+                turn += 1
 
     def remote(src, dst, send, recv, device):
         return pltpu.make_async_remote_copy(
@@ -280,17 +305,21 @@
     ]
     for copy in own_tables:
         copy.start()
-    pl.semaphore_wait(barrier, total)
+    pl.semaphore_wait(barrier, 7)
     lanes = [(side, hop) for hop in range(GROUPS) for side in range(2) if hop < len(CAPS[side])]
-    for part in range(2):
-        for side in range(2):
-            hop_copy(side, 0, part).start()
+    for side in range(2):
+        hop_copy(side, 0, 0).start()
+    meet()
     for side, hop in lanes:
         for copy in table_copies(side, hop):
             copy.start()
-    weight_copies = [to_partner(0, wg_ref, xg), to_partner(1, wu_ref, xu), to_partner(2, wd_ref, xd)]
+    for copy in weight_loads:
+        copy.wait()
+    weight_copies = [to_partner(0, wg, xg), to_partner(1, wu, xu), to_partner(2, wd, xd)]
     for copy in weight_copies:
         copy.start()
+    for side in range(2):
+        hop_copy(side, 0, 1).start()
     for copy in own_tables:
         copy.wait()
 
@@ -312,10 +341,10 @@
     pick(GROUPS - 1, 1)
     send_blocks(GROUPS - 1, 1)
 
-    gh[:, :half], gl[:, :half] = split(wg_ref[...])
-    uh[:, :half], ul[:, :half] = split(wu_ref[...])
-    dh[:half, :], dl[:half, :] = split(wd_ref[...])
-    for ref in (og_ref, ou_ref, od_ref, ag, au, ad):
+    gh[:, :half], gl[:, :half] = split(wg[...])
+    uh[:, :half], ul[:, :half] = split(wu[...])
+    dh[:half, :], dl[:half, :] = split(wd[...])
+    for ref in (og, ou, od, ag, au, ad):
         ref[...] = jnp.zeros_like(ref)
     for copy in weight_copies:
         copy.wait()
@@ -377,9 +406,9 @@
         ag[...] += d_gg[:, half:]
         au[...] += d_uu[:, half:]
         ad[...] += d_dd[half:, :]
-        og_ref[...] += d_gg[:, :half]
-        ou_ref[...] += d_uu[:, :half]
-        od_ref[...] += d_dd[:half, :]
+        og[...] += d_gg[:, :half]
+        ou[...] += d_uu[:, :half]
+        od[...] += d_dd[:half, :]
 
         own_block = (GROUPS - 1) * per_group + plane
 
@@ -421,11 +450,17 @@
     grad_copies = [to_partner(3, ag, rg), to_partner(4, au, ru), to_partner(5, ad, rd)]
     for copy in grad_copies:
         copy.start()
-    for copy, out, got in zip(grad_copies, (og_ref, ou_ref, od_ref), (rg, ru, rd)):
+    for copy, out, got in zip(grad_copies, (og, ou, od), (rg, ru, rd)):
         copy.wait()
         out[...] += got[...]
 
     pltpu.make_async_copy(bbuf, bbuf, back_recv_sem).wait()
+    stores = [
+        pltpu.make_async_copy(src, dst, load_sem.at[i])
+        for i, (src, dst) in enumerate([(og, og_ref), (ou, ou_ref), (od, od_ref)])
+    ]
+    for copy in stores:
+        copy.start()
 
     flat_back = bbuf.reshape(total * MOST, SUB, LANES)
 
@@ -441,6 +476,8 @@
     for lane in range(SUB):
         gx_ref[:, pl.ds(lane * LANES, LANES)] = flat_tok[pl.ds(lane, tokens, stride=SUB), :]
 
+    for copy in stores:
+        copy.wait()
     for side, hop in lanes:
         for part in range(len(hop_parts(side, hop))):
             hop_copy(side, hop, part).wait_send()
@@ -452,6 +489,25 @@
     pltpu.make_async_copy(tbuf.at[others], tbuf.at[others], back_send_sem).wait()
 
 
+def settle(*refs):
+    ins, outs, held, (load, store) = refs[:4], refs[4:8], refs[8:12], refs[12:]
+    loads, stores = [], []
+    for i, (src, dst, mid) in enumerate(zip(ins, outs, held)):
+        rows = mid.shape[0] // 2
+        for part in range(2):
+            at = pl.ds(part * rows, rows)
+            loads.append(pltpu.make_async_copy(src.at[at], mid.at[at], load.at[i, part]))
+            to = dst.at[at] if i == 0 else dst.at[0, at]
+            stores.append(pltpu.make_async_copy(mid.at[at], to, store.at[i, part]))
+    for copy in loads:
+        copy.start()
+    for first, second in zip(loads, stores):
+        first.wait()
+        second.start()
+    for copy in stores:
+        copy.wait()
+
+
 def local(nx, ny, nz, tokens, cotangent, w_gate, w_up, w_down, expert_ids, route_weight, halted):
     token_count, width = tokens.shape
     half = w_gate.shape[2]
@@ -460,6 +516,7 @@
     rows = 2 * plane * MOST
     tile = (SUB, LANES)
     vmem = pl.BlockSpec(memory_space=pltpu.VMEM)
+    hbm = pl.BlockSpec(memory_space=pl.ANY)
     dma = pltpu.SemaphoreType.DMA
     grad_x, g_gate, g_upper, g_down = pl.pallas_call(
         functools.partial(kernel, nx, ny, nz),
@@ -469,9 +526,15 @@
             jax.ShapeDtypeStruct((width, half), F32),
             jax.ShapeDtypeStruct((half, width), F32),
         ),
-        in_specs=[vmem] * 8,
-        out_specs=(vmem,) * 4,
+        in_specs=[vmem] * 5 + [hbm] * 3,
+        out_specs=(vmem,) + (hbm,) * 3,
         scratch_shapes=[
+            pltpu.VMEM((width, half), F32),
+            pltpu.VMEM((width, half), F32),
+            pltpu.VMEM((half, width), F32),
+            pltpu.VMEM((width, half), F32),
+            pltpu.VMEM((width, half), F32),
+            pltpu.VMEM((half, width), F32),
             pltpu.VMEM((token_count,) + tile, F32),
             pltpu.VMEM((token_count,) + tile, F32),
             pltpu.VMEM(tile, jnp.int32),
@@ -510,6 +573,8 @@
             pltpu.VMEM((rows, width), BF16),
             pltpu.VMEM((rows, width), BF16),
             pltpu.VMEM((rows, width), BF16),
+            dma((3,)),
+            pltpu.SemaphoreType.REGULAR((nz // 2 - 1 + nx // 2 + ny // 2,)),
             dma((2, GROUPS, 2)),
             dma((2, GROUPS, 2)),
             dma((2 * GROUPS,)),
@@ -537,7 +602,15 @@
         w_up[0],
         w_down[0],
     )
-    return grad_x, g_gate[None], g_upper[None], g_down[None]
+    arrays = (grad_x, g_gate, g_upper, g_down)
+    return pl.pallas_call(
+        settle,
+        out_shape=(jax.ShapeDtypeStruct(grad_x.shape, F32),)
+        + tuple(jax.ShapeDtypeStruct((1,) + array.shape, F32) for array in arrays[1:]),
+        in_specs=[hbm] * 4,
+        out_specs=(hbm,) * 4,
+        scratch_shapes=[pltpu.VMEM(array.shape, F32) for array in arrays] + [dma((4, 2)), dma((4, 2))],
+    )(*arrays)
 
 
 def solution(mesh):

time: 138 us -> 126 us (0.913)
  the two profiles are of different devices: /device:TPU:33 before, /device:TPU:1 now
where the time goes in v3:
time: 126 us; the launch traced here: 124 us
  Pallas kernels  124 us (98%)
    pallas_call x1, Pallas kernels, local(): pl.pallas_call(functools.partial(kernel, nx, ny, nz), out_shape=(jax.Shap...  121 us
    pallas_call x1, Pallas kernels, local(): pl.pallas_call(settle, out_shape=(jax.ShapeDtypeStruct(grad_x.shape, F32)...  3.26 us

profile of v3, /device:TPU:1, one launch (start us, length us, event | category | flops | bytes accessed | tf_op | source)
XLA Modules:
  0.0 124.4 jit_solution(11394086986245870607)
XLA Ops:
  0.6 120.5 %shard_map.111 = (f32[128,1024]{1,0:T(8,128)}, f32[1024,256]{1,0:T(8,128)}, f32[1024,256]{1,0:T(8,128)}, f32[256,1024]{1,0:T(8,128)}) custom-call(s32[2,128]{1,0:T(2,128)} %bitcast.9, f32[2,128]{1,0:T(2,128)} %bitcast.10, s32[1,128]{1,0:T(1,128)} %bitcast.11, f32[128,1024]{1,0:T(8,128)} %tok_ref.1, f32[128,1024]{1,0:T(8,128)} %cot_ref.1, ...), custom_call_target="tpu_custom_call" | custom-call | tf_op jit(solution)/shard_map/pallas_call | solution.py:521
  121.2 3.3 %shard_map.112 = (f32[128,1024]{1,0:T(8,128)}, f32[1,1024,256]{2,1,0:T(8,128)}, f32[1,1024,256]{2,1,0:T(8,128)}, f32[1,256,1024]{2,1,0:T(8,128)}) custom-call(f32[128,1024]{1,0:T(8,128)} %get-tuple-element.8.refs_0_, f32[1024,256]{1,0:T(8,128)} %get-tuple-element.9.refs_1_, f32[1024,256]{1,0:T(8,128)} %get-tuple-element.10.refs_2_, ...), custom_call_target="tpu_custom_call" | custom-call | tf_op jit(solution)/shard_map/pallas_call | solution.py:606

commit v4 on v3

--- a/solution.py
+++ b/solution.py
@@ -11,7 +11,8 @@
 MOST = 3
 GROUPS = 4
 FIRST = 48
-CAPS = ((128, 128, 96, 48), (128, 96, 48))
+BOUNDS = ((128, 128, 96, 48), (128, 96, 48))
+USUAL = ((112, 96, 80, 48), (96, 80, 48))
 LANES = 128
 SUB = 8
 F32 = jnp.float32
@@ -31,6 +32,7 @@
 
 
 def kernel(
+    caps,
     nx,
     ny,
     nz,
@@ -46,6 +48,7 @@
     og_ref,
     ou_ref,
     od_ref,
+    flag_ref,
     wg,
     wu,
     wd,
@@ -59,6 +62,9 @@
     turn_w,
     list_v,
     list_s,
+    flag_in,
+    flag_out,
+    flag_pair,
     row_ref,
     wgt_ref,
     own,
@@ -103,6 +109,8 @@
     recv_sem,
     back_send_sem,
     back_recv_sem,
+    flag_send_sem,
+    flag_recv_sem,
     pair_send_sem,
     pair_recv_sem,
 ):
@@ -174,7 +182,7 @@
         return column(sign if side == 0 else -sign)
 
     def hop_parts(side, hop):
-        cap = CAPS[side][hop]
+        cap = caps[side][hop]
         return ((0, FIRST), (FIRST, cap)) if cap > FIRST else ((0, cap),)
 
     def hop_copy(side, hop, part):
@@ -254,6 +262,12 @@
         other = column_of(columns, i)
         places.append(count((other > lines[i]) | ((other == lines[i]) & earlier)))
     lane_index = lax.broadcasted_iota(jnp.int32, (1, tokens), 1)
+    over = jnp.zeros((1, 1), jnp.int32)
+    for side in range(2):
+        for hop, cap in enumerate(caps[side]):
+            needed = jnp.sum(jnp.where(far[side] > hop, 1, 0), axis=1, keepdims=True)
+            over += jnp.where(needed > cap, 1, 0)
+    flag_lane = lane_index == LANES - 1
     shift = nz.bit_length() - 1
     for i in range(2):
         turn_b[pl.ds(i, 1), :] = places[i]
@@ -284,9 +298,9 @@
         wgt = jnp.sum(
             sum(jnp.where(hit[j], column_of(weights, j), 0.0) for j in range(2)), axis=0, keepdims=True
         )
-        limit = CAPS[i % 2][i // 2] if i // 2 < len(CAPS[i % 2]) else tokens
+        limit = caps[i % 2][i // 2] if i // 2 < len(caps[i % 2]) else tokens
         row_ref[i] = jnp.broadcast_to(jnp.clip(row, 0, limit - 1), (SUB, LANES))
-        wgt_ref[i] = jnp.broadcast_to(wgt, (SUB, LANES))
+        wgt_ref[i] = jnp.broadcast_to(jnp.where(flag_lane, over.astype(F32), wgt), (SUB, LANES))
     pick_lists.wait()
 
     @pl.loop(0, tokens // SUB)
@@ -306,7 +320,7 @@
     for copy in own_tables:
         copy.start()
     pl.semaphore_wait(barrier, 7)
-    lanes = [(side, hop) for hop in range(GROUPS) for side in range(2) if hop < len(CAPS[side])]
+    lanes = [(side, hop) for hop in range(GROUPS) for side in range(2) if hop < len(caps[side])]
     for side in range(2):
         hop_copy(side, 0, 0).start()
     meet()
@@ -355,7 +369,7 @@
         for copy in table_copies(side, hop):
             copy.wait_recv()
     tables = [
-        pltpu.make_async_copy(table.at[side, pl.ds(0, len(CAPS[side]))], to.at[side, pl.ds(0, len(CAPS[side]))], tab_sem.at[i])
+        pltpu.make_async_copy(table.at[side, pl.ds(0, len(caps[side]))], to.at[side, pl.ds(0, len(caps[side]))], tab_sem.at[i])
         for i, (table, to, side) in enumerate(
             [(row_in, row_tab, 0), (wgt_in, wgt_tab, 0), (row_in, row_tab, 1), (wgt_in, wgt_tab, 1)]
         )
@@ -364,6 +378,14 @@
         copy.start()
     for copy in tables:
         copy.wait()
+
+    in_column = wgt_ref[0]
+    for side, hop in lanes:
+        in_column += wgt_in[side, hop]
+    flag_out[0] = in_column
+
+    def flag_copy(cell):
+        return remote(flag_out.at[0], flag_in.at[cell], flag_send_sem, flag_recv_sem, beside(cell))
 
     flat_in = rbuf.reshape(total * 2 * MOST * SUB, LANES)
     flat_out = tbuf.reshape(total * MOST * SUB, LANES)
@@ -424,6 +446,10 @@
             def _():
                 pltpu.make_async_copy(tbuf.at[own_block], bbuf.at[own_block], back_recv_sem).start()
 
+    @pl.loop(1, plane)
+    def _(cell):
+        flag_copy(cell).start()
+
     @pl.loop(0, GROUPS + 1)
     def _(step):
         for hop in range(GROUPS):
@@ -431,22 +457,29 @@
             @pl.when(step == hop)
             def _():
                 for side in range(2):
-                    if hop < len(CAPS[side]):
+                    if hop < len(caps[side]):
                         for part in range(len(hop_parts(side, hop))):
                             hop_copy(side, hop, part).wait_recv()
-                            if hop + 1 < len(CAPS[side]) and part < len(hop_parts(side, hop + 1)):
+                            if hop + 1 < len(caps[side]) and part < len(hop_parts(side, hop + 1)):
                                 hop_copy(side, hop + 1, part).start()
                 for side in range(2):
-                    if hop < len(CAPS[side]):
+                    if hop < len(caps[side]):
                         pick(hop, side)
                 for side in range(2):
-                    if hop < len(CAPS[side]):
+                    if hop < len(caps[side]):
                         send_blocks(hop, side)
 
         @pl.when(step >= 1)
         def _():
             compute(step - 1)
 
+    other_flags = flag_in.at[pl.ds(1, plane - 1)]
+    pltpu.make_async_copy(other_flags, other_flags, flag_recv_sem).wait()
+    pltpu.make_async_copy(other_flags, other_flags, flag_send_sem).wait()
+    in_core = flag_out[0]
+    for cell in range(1, plane):
+        in_core += flag_in[cell]
+    flag_out[1] = in_core
     grad_copies = [to_partner(3, ag, rg), to_partner(4, au, ru), to_partner(5, ad, rd)]
     for copy in grad_copies:
         copy.start()
@@ -454,7 +487,11 @@
         copy.wait()
         out[...] += got[...]
 
+    flag_swap = to_partner(6, flag_out.at[1], flag_pair)
+    flag_swap.start()
     pltpu.make_async_copy(bbuf, bbuf, back_recv_sem).wait()
+    flag_swap.wait()
+    flag_ref[...] = flag_out[1] + flag_pair[...]
     stores = [
         pltpu.make_async_copy(src, dst, load_sem.at[i])
         for i, (src, dst) in enumerate([(og, og_ref), (ou, ou_ref), (od, od_ref)])
@@ -518,99 +555,115 @@
     vmem = pl.BlockSpec(memory_space=pltpu.VMEM)
     hbm = pl.BlockSpec(memory_space=pl.ANY)
     dma = pltpu.SemaphoreType.DMA
-    grad_x, g_gate, g_upper, g_down = pl.pallas_call(
-        functools.partial(kernel, nx, ny, nz),
-        out_shape=(
-            jax.ShapeDtypeStruct((token_count, width), F32),
-            jax.ShapeDtypeStruct((width, half), F32),
-            jax.ShapeDtypeStruct((width, half), F32),
-            jax.ShapeDtypeStruct((half, width), F32),
-        ),
-        in_specs=[vmem] * 5 + [hbm] * 3,
-        out_specs=(vmem,) + (hbm,) * 3,
-        scratch_shapes=[
-            pltpu.VMEM((width, half), F32),
-            pltpu.VMEM((width, half), F32),
-            pltpu.VMEM((half, width), F32),
-            pltpu.VMEM((width, half), F32),
-            pltpu.VMEM((width, half), F32),
-            pltpu.VMEM((half, width), F32),
-            pltpu.VMEM((token_count,) + tile, F32),
-            pltpu.VMEM((token_count,) + tile, F32),
-            pltpu.VMEM(tile, jnp.int32),
-            pltpu.VMEM(tile, jnp.int32),
-            pltpu.VMEM(tile, F32),
-            pltpu.VMEM(tile, jnp.int32),
-            pltpu.SMEM(tile, jnp.int32),
-            pltpu.VMEM((2 * GROUPS,) + tile, jnp.int32),
-            pltpu.VMEM((2 * GROUPS,) + tile, F32),
-            pltpu.VMEM((2, token_count, 2) + tile, F32),
-            tuple(tuple(pltpu.VMEM((cap, 2) + tile, F32) for cap in caps) for caps in CAPS),
-            pltpu.VMEM((2, GROUPS) + tile, jnp.int32),
-            pltpu.VMEM((2, GROUPS) + tile, F32),
-            pltpu.SMEM((2, GROUPS) + tile, jnp.int32),
-            pltpu.SMEM((2, GROUPS) + tile, F32),
-            pltpu.VMEM((total, 2 * MOST) + tile, F32),
-            pltpu.VMEM((total, 2 * MOST) + tile, F32),
-            pltpu.VMEM((total, MOST) + tile, F32),
-            pltpu.VMEM((total, MOST) + tile, F32),
-            pltpu.VMEM((width, half), F32),
-            pltpu.VMEM((width, half), F32),
-            pltpu.VMEM((half, width), F32),
-            pltpu.VMEM((width, 2 * half), BF16),
-            pltpu.VMEM((width, 2 * half), BF16),
-            pltpu.VMEM((width, 2 * half), BF16),
-            pltpu.VMEM((width, 2 * half), BF16),
-            pltpu.VMEM((2 * half, width), BF16),
-            pltpu.VMEM((2 * half, width), BF16),
-            pltpu.VMEM((width, half), F32),
-            pltpu.VMEM((width, half), F32),
-            pltpu.VMEM((half, width), F32),
-            pltpu.VMEM((width, half), F32),
-            pltpu.VMEM((width, half), F32),
-            pltpu.VMEM((half, width), F32),
-            pltpu.VMEM((rows, width), BF16),
-            pltpu.VMEM((rows, width), BF16),
-            pltpu.VMEM((rows, width), BF16),
-            pltpu.VMEM((rows, width), BF16),
-            dma((3,)),
-            pltpu.SemaphoreType.REGULAR((nz // 2 - 1 + nx // 2 + ny // 2,)),
-            dma((2, GROUPS, 2)),
-            dma((2, GROUPS, 2)),
-            dma((2 * GROUPS,)),
-            dma((2, GROUPS)),
-            dma((2 * GROUPS,)),
-            dma((2, GROUPS)),
-            dma((4,)),
-            dma,
-            dma((GROUPS,)),
-            dma,
-            dma,
-            dma((6,)),
-            dma((6,)),
-        ],
-        compiler_params=pltpu.CompilerParams(
-            collective_id=0, has_side_effects=True, vmem_limit_bytes=63 * 1024 * 1024
-        ),
-    )(
-        expert_ids.T,
-        route_weight.T,
-        halted.reshape(1, token_count),
-        tokens,
-        cotangent,
-        w_gate[0],
-        w_up[0],
-        w_down[0],
+    def layer(caps, number):
+        return pl.pallas_call(
+            functools.partial(kernel, caps, nx, ny, nz),
+            out_shape=(
+                jax.ShapeDtypeStruct((token_count, width), F32),
+                jax.ShapeDtypeStruct((width, half), F32),
+                jax.ShapeDtypeStruct((width, half), F32),
+                jax.ShapeDtypeStruct((half, width), F32),
+                jax.ShapeDtypeStruct(tile, F32),
+            ),
+            in_specs=[vmem] * 5 + [hbm] * 3,
+            out_specs=(vmem,) + (hbm,) * 3 + (vmem,),
+            scratch_shapes=[
+                pltpu.VMEM((width, half), F32),
+                pltpu.VMEM((width, half), F32),
+                pltpu.VMEM((half, width), F32),
+                pltpu.VMEM((width, half), F32),
+                pltpu.VMEM((width, half), F32),
+                pltpu.VMEM((half, width), F32),
+                pltpu.VMEM((token_count,) + tile, F32),
+                pltpu.VMEM((token_count,) + tile, F32),
+                pltpu.VMEM(tile, jnp.int32),
+                pltpu.VMEM(tile, jnp.int32),
+                pltpu.VMEM(tile, F32),
+                pltpu.VMEM(tile, jnp.int32),
+                pltpu.SMEM(tile, jnp.int32),
+                pltpu.VMEM((plane,) + tile, F32),
+                pltpu.VMEM((2,) + tile, F32),
+                pltpu.VMEM(tile, F32),
+                pltpu.VMEM((2 * GROUPS,) + tile, jnp.int32),
+                pltpu.VMEM((2 * GROUPS,) + tile, F32),
+                pltpu.VMEM((2, token_count, 2) + tile, F32),
+                tuple(tuple(pltpu.VMEM((cap, 2) + tile, F32) for cap in side) for side in caps),
+                pltpu.VMEM((2, GROUPS) + tile, jnp.int32),
+                pltpu.VMEM((2, GROUPS) + tile, F32),
+                pltpu.SMEM((2, GROUPS) + tile, jnp.int32),
+                pltpu.SMEM((2, GROUPS) + tile, F32),
+                pltpu.VMEM((total, 2 * MOST) + tile, F32),
+                pltpu.VMEM((total, 2 * MOST) + tile, F32),
+                pltpu.VMEM((total, MOST) + tile, F32),
+                pltpu.VMEM((total, MOST) + tile, F32),
+                pltpu.VMEM((width, half), F32),
+                pltpu.VMEM((width, half), F32),
+                pltpu.VMEM((half, width), F32),
+                pltpu.VMEM((width, 2 * half), BF16),
+                pltpu.VMEM((width, 2 * half), BF16),
+                pltpu.VMEM((width, 2 * half), BF16),
+                pltpu.VMEM((width, 2 * half), BF16),
+                pltpu.VMEM((2 * half, width), BF16),
+                pltpu.VMEM((2 * half, width), BF16),
+                pltpu.VMEM((width, half), F32),
+                pltpu.VMEM((width, half), F32),
+                pltpu.VMEM((half, width), F32),
+                pltpu.VMEM((width, half), F32),
+                pltpu.VMEM((width, half), F32),
+                pltpu.VMEM((half, width), F32),
+                pltpu.VMEM((rows, width), BF16),
+                pltpu.VMEM((rows, width), BF16),
+                pltpu.VMEM((rows, width), BF16),
+                pltpu.VMEM((rows, width), BF16),
+                dma((3,)),
+                pltpu.SemaphoreType.REGULAR((nz // 2 - 1 + nx // 2 + ny // 2,)),
+                dma((2, GROUPS, 2)),
+                dma((2, GROUPS, 2)),
+                dma((2 * GROUPS,)),
+                dma((2, GROUPS)),
+                dma((2 * GROUPS,)),
+                dma((2, GROUPS)),
+                dma((4,)),
+                dma,
+                dma((GROUPS,)),
+                dma,
+                dma,
+                dma,
+                dma,
+                dma((7,)),
+                dma((7,)),
+            ],
+            compiler_params=pltpu.CompilerParams(
+                collective_id=number, has_side_effects=True, vmem_limit_bytes=63 * 1024 * 1024
+            ),
+        )(
+            expert_ids.T,
+            route_weight.T,
+            halted.reshape(1, token_count),
+            tokens,
+            cotangent,
+            w_gate[0],
+            w_up[0],
+            w_down[0],
+        )
+
+    def settled(arrays):
+        return pl.pallas_call(
+            settle,
+            out_shape=(jax.ShapeDtypeStruct(arrays[0].shape, F32),)
+            + tuple(jax.ShapeDtypeStruct((1,) + array.shape, F32) for array in arrays[1:]),
+            in_specs=[hbm] * 4,
+            out_specs=(hbm,) * 4,
+            scratch_shapes=[pltpu.VMEM(array.shape, F32) for array in arrays] + [dma((4, 2)), dma((4, 2))],
+        )(*arrays)
+
+    *arrays, flag = layer(USUAL, 0)
+    return lax.cond(
+        flag[0, LANES - 1] > 0.0,
+        lambda _: settled(layer(BOUNDS, 1)[:4]),
+        settled,
+        tuple(arrays),
     )
-    arrays = (grad_x, g_gate, g_upper, g_down)
-    return pl.pallas_call(
-        settle,
-        out_shape=(jax.ShapeDtypeStruct(grad_x.shape, F32),)
-        + tuple(jax.ShapeDtypeStruct((1,) + array.shape, F32) for array in arrays[1:]),
-        in_specs=[hbm] * 4,
-        out_specs=(hbm,) * 4,
-        scratch_shapes=[pltpu.VMEM(array.shape, F32) for array in arrays] + [dma((4, 2)), dma((4, 2))],
-    )(*arrays)
 
 
 def solution(mesh):

time: 126 us -> 120 us (0.952)
  Pallas kernels: 124 us -> 115 us
  local copies, waits for them, and re-layouts: 0 us -> 1.92 us
    pallas_call x2, Pallas kernels: 124 us -> 115 us  [the longest x1 112 us: layer(): pl.pallas_call(functools.partial(kernel, caps, nx, ny, nz), out_shape=(ja...]
where the time goes in v4:
time: 120 us; the launch traced here: 119 us
  Pallas kernels  115 us (96%)
  local copies, waits for them, and re-layouts  1.92 us (2%)
  between operations  1.49 us (1%)
    pallas_call x1, Pallas kernels, layer(): pl.pallas_call(functools.partial(kernel, caps, nx, ny, nz), out_shape=(ja...  112 us
    pallas_call x1, Pallas kernels, settled(): pl.pallas_call(settle, out_shape=(jax.ShapeDtypeStruct(arrays[0].shape, F...  3.26 us

profile of v4, /device:TPU:1, one launch (start us, length us, event | category | flops | bytes accessed | tf_op | source)
XLA Modules:
  0.0 118.6 jit_solution(12398734787823305330)
XLA Ops:
  0.6 0.0 copy-start.2
  0.6 0.0 copy-start.1
  0.7 0.0 copy-start.3
  0.7 0.7 copy-done.2
  1.3 0.0 copy-done.1
  1.3 0.0 copy-done.3
  1.3 0.0 copy-start
  1.3 111.8 %shard_map.119 = (f32[128,1024]{1,0:T(8,128)}, f32[1024,256]{1,0:T(8,128)}, f32[1024,256]{1,0:T(8,128)}, f32[256,1024]{1,0:T(8,128)}, f32[8,128]{1,0:T(8,128)}) custom-call(s32[2,128]{1,0:T(2,128)S(1)} %bitcast.19, f32[2,128]{1,0:T(2,128)S(1)} %bitcast.21, s32[1,128]{1,0:T(1,128)S(1)} %bitcast.23, f32[128,1024]{1,0:T(8,128)} %tok_ref.1, ...), custom_call_target="tpu_custom_call" | custom-call | tf_op jit(solution)/shard_map/pallas_call | solution.py:559
  113.1 1.2 %slice.3 = f32[1,1]{1,0:T(1,128)} slice(f32[8,128]{1,0:T(8,128)} %get-tuple-element.49), slice={[0:1], [127:128]} | slice | bytes 8 | tf_op jit(solution)/shard_map/slice | solution.py:662
  115.0 0.0 copy-done
  115.0 3.5 %conditional.1 = ((f32[128,1024]{1,0:T(8,128)}, f32[1,1024,256]{2,1,0:T(8,128)}, f32[1,1024,256]{2,1,0:T(8,128)}, f32[1,256,1024]{2,1,0:T(8,128)})) conditional(s32[]{:T(128)} %bitcast.12, (f32[128,1024]{1,0:T(8,128)}, f32[1024,256]{1,0:T(8,128)}, f32[1024,256]{1,0:T(8,128)}, f32[256,1024]{1,0:T(8,128)}) %tuple.13, (s32[128,2]{0,1:T(2,128)S(1)}, ...), branch_computations={%region_0.0_spmd, %region_1.0_spmd} | conditional | bytes 8 | solution.py:661
  115.0 3.3 %branch_0_fun.1 = (f32[128,1024]{1,0:T(8,128)}, f32[1,1024,256]{2,1,0:T(8,128)}, f32[1,1024,256]{2,1,0:T(8,128)}, f32[1,256,1024]{2,1,0:T(8,128)}) custom-call(f32[128,1024]{1,0:T(8,128)} %get-tuple-element.24.refs_0_, f32[1024,256]{1,0:T(8,128)} %get-tuple-element.25.refs_1_, f32[1024,256]{1,0:T(8,128)} %get-tuple-element.26.refs_2_, ...), custom_call_target="tpu_custom_call" | custom-call | tf_op jit(solution)/shard_map/cond/branch_0_fun/pallas_call | solution.py:651
Async XLA Ops:
  0.6 0.7 copy-start.2
  0.6 0.7 copy-start.1
  0.7 0.7 copy-start.3
  1.3 113.7 %copy-start = (f32[128,1024]{1,0:T(8,128)S(1)}, f32[128,1024]{1,0:T(8,128)}, u32[]{:S(2)}) copy-start(f32[128,1024]{1,0:T(8,128)} %tok_ref.1) | copy-start | bytes 1572868
